TPU v7x, 32 devices: a whole 2x2x4 slice. The times are simulated.
32 devices in a mesh: dp: 8 (over z, y), mp: 4 (over x, core).
Axes of the slice: x: 2, y: 2, z: 4, core: 2. Of those that a mesh axis runs over, the one named last changes fastest.
Arguments:
- tokens: bfloat16 [16, 2048, 768], P('dp', 'mp'), may hold values from -6 to 6
- lengths: int32 [16], replicated, may hold values from 1 to 2048, as said below
- order: int32 [16], replicated, may hold values from 0 to 15, as said below
- q_weight: bfloat16 [768, 768], P(('dp', 'mp')), may hold values from -0.21875 to 0.21875
- k_weight: bfloat16 [768, 768], P(('dp', 'mp')), may hold values from -0.21875 to 0.21875
- v_weight: bfloat16 [768, 768], P(('dp', 'mp')), may hold values from -0.21875 to 0.21875
- o_weight: bfloat16 [768, 768], P(('dp', 'mp')), may hold values from -6 to 6
- q_bias: bfloat16 [768], P(('dp', 'mp')), may hold values from -1.1953125 to 1.1953125
- v_bias: bfloat16 [768], P(('dp', 'mp')), may hold values from -0.059814453 to 0.059814453
- o_bias: bfloat16 [768], P(('dp', 'mp')), may hold values from -1.1953125 to 1.1953125
- attn_gain: bfloat16 [768], P(('dp', 'mp')), may hold values from 0.5 to 1.5
- attn_shift: bfloat16 [768], P(('dp', 'mp')), may hold values from -1.1953125 to 1.1953125
- in_weight: bfloat16 [768, 3072], P(('dp', 'mp')), may hold values from -0.21875 to 0.21875
- in_bias: bfloat16 [3072], P(('dp', 'mp')), may hold values from -1.1953125 to 1.1953125
- out_weight: bfloat16 [3072, 768], P(('dp', 'mp')), may hold values from -0.109375 to 0.109375
- out_bias: bfloat16 [768], P(('dp', 'mp')), may hold values from -1.1953125 to 1.1953125
- ffn_gain: bfloat16 [768], P(('dp', 'mp')), may hold values from 0.5 to 1.5
- ffn_shift: bfloat16 [768], P(('dp', 'mp')), may hold values from -1.1953125 to 1.1953125
- cotangent: bfloat16 [16, 2048, 768], P('dp', 'mp'), may hold values from -6 to 6
Outputs:
- output: bfloat16 [16, 2048, 768], P('dp', 'mp')
- input_grad: float32 [16, 2048, 768], P('dp', 'mp')
- q_weight_grad: float32 [768, 768], P(('dp', 'mp'))
- k_weight_grad: float32 [768, 768], P(('dp', 'mp'))
- v_weight_grad: float32 [768, 768], P(('dp', 'mp'))
- o_weight_grad: float32 [768, 768], P(('dp', 'mp'))
- q_bias_grad: float32 [768], P(('dp', 'mp'))
- v_bias_grad: float32 [768], P(('dp', 'mp'))
- o_bias_grad: float32 [768], P(('dp', 'mp'))
- attn_gain_grad: float32 [768], P(('dp', 'mp'))
- attn_shift_grad: float32 [768], P(('dp', 'mp'))
- in_weight_grad: float32 [768, 3072], P(('dp', 'mp'))
- in_bias_grad: float32 [3072], P(('dp', 'mp'))
- out_weight_grad: float32 [3072, 768], P(('dp', 'mp'))
- out_bias_grad: float32 [768], P(('dp', 'mp'))
- ffn_gain_grad: float32 [768], P(('dp', 'mp'))
- ffn_shift_grad: float32 [768], P(('dp', 'mp'))
Inputs may be any that keep to these rules, and one draw needn't show every extreme that they name: `lengths`: some sequence has exactly 2048 live positions. `order`: A permutation of the 16 sequences.
All inputs are finite; a program needn't handle non-finite values.
Results may differ from a plain program's by a relative error of at most 0.018.
Values may be sent and summed in bfloat16 or wider, within the bound.
A program may use at most 192 MiB of HBM per device.

v0:
```python
import jax
import jax.numpy as jnp
from jax import lax
from jax.sharding import PartitionSpec as P

H = 12
HD = 64


epsilon = 1e-05
root_half = 0.7071067811865476
inverse_root_two_pi = 0.3989422804014327


def norm_forward(values, gain, shift):
    center = jnp.mean(values, axis=-1, keepdims=True)
    offset = values - center
    inverse = lax.rsqrt(jnp.mean(offset * offset, axis=-1, keepdims=True) + epsilon)
    normed = offset * inverse
    return (normed * gain + shift, normed, inverse)


def norm_backward(gradient, normed, inverse, gain):
    scaled = gradient * gain
    centered = (
        scaled
        - jnp.mean(scaled, axis=-1, keepdims=True)
        - normed * jnp.mean(scaled * normed, axis=-1, keepdims=True)
    )
    return (inverse * centered, jnp.sum(gradient * normed, axis=0), jnp.sum(gradient, axis=0))


def split_heads(values):
    return values.reshape(values.shape[0], H, HD).transpose(1, 0, 2)


def merge_heads(values):
    return values.transpose(1, 0, 2).reshape(values.shape[1], H * HD)


def head_scores(head_q, head_k, visible):
    scores = jnp.einsum("qd,kd->qk", head_q, head_k, preferred_element_type=jnp.float32) * 0.125
    return jnp.where(visible[None, :], scores, -1e30)


def attend(queries, key_rows, value_rows, visible):

    def per_head(members):
        head_q, head_k, head_v = members
        scores = head_scores(head_q, head_k, visible)
        top_score = jnp.max(scores, axis=-1, keepdims=True)
        raised = jnp.exp(scores - top_score)
        denominator = jnp.sum(raised, axis=-1, keepdims=True)
        shares = (raised / denominator).astype(jnp.bfloat16)
        context = jnp.dot(shares, head_v, preferred_element_type=jnp.float32)
        return (context, (top_score + jnp.log(denominator))[:, 0])

    context, log_totals = lax.map(
        per_head, (split_heads(queries), split_heads(key_rows), split_heads(value_rows))
    )
    return (merge_heads(context), log_totals)


def attend_back(queries, key_rows, value_rows, visible, log_totals, grad_context):

    def per_head(members):
        head_q, head_k, head_v, head_total, head_grad = members
        shares = jnp.exp(head_scores(head_q, head_k, visible) - head_total[:, None])
        share_low = shares.astype(jnp.bfloat16)
        grad_shares = jnp.einsum("qd,kd->qk", head_grad, head_v, preferred_element_type=jnp.float32)
        grad_v = jnp.einsum("qk,qd->kd", share_low, head_grad, preferred_element_type=jnp.float32)
        weighted = jnp.sum(shares * grad_shares, axis=-1, keepdims=True)
        grad_scores = (shares * (grad_shares - weighted)).astype(jnp.bfloat16)
        grad_q = jnp.dot(grad_scores, head_k, preferred_element_type=jnp.float32) * 0.125
        grad_k = (
            jnp.einsum("qk,qd->kd", grad_scores, head_q, preferred_element_type=jnp.float32) * 0.125
        )
        return (grad_q, grad_k, grad_v)

    grad_q, grad_k, grad_v = lax.map(
        per_head,
        (
            split_heads(queries),
            split_heads(key_rows),
            split_heads(value_rows),
            log_totals,
            split_heads(grad_context),
        ),
    )
    return (merge_heads(grad_q), merge_heads(grad_k), merge_heads(grad_v))


def deal_rows(tokens, order):
    micro_count, rows, width = tokens.shape
    groups = lax.axis_size("dp")
    piece_rows = rows // groups
    pieces = tokens.reshape(micro_count, groups, piece_rows, width)
    mixed = lax.all_to_all(pieces, "dp", split_axis=1, concat_axis=0, tiled=True)
    every_seq = mixed.reshape(groups * micro_count, piece_rows, width)
    picked = jnp.take(every_seq, order, axis=0)
    outgoing = picked.reshape(groups, micro_count, piece_rows, width)
    joined = lax.all_to_all(outgoing, "dp", split_axis=0, concat_axis=2, tiled=True)
    return joined.reshape(micro_count, rows, width)


def forward(whole, inputs, length):
    (
        q_weight,
        k_weight,
        v_weight,
        o_weight,
        q_bias,
        v_bias,
        o_bias,
        attn_gain,
        attn_shift,
        in_weight,
        in_bias,
        out_weight,
        out_bias,
        ffn_gain,
        ffn_shift,
    ) = whole
    queries = (jnp.dot(inputs, q_weight, preferred_element_type=jnp.float32) + q_bias).astype(
        jnp.bfloat16
    )
    key_part = jnp.dot(inputs, k_weight, preferred_element_type=jnp.float32).astype(jnp.bfloat16)
    value_part = (jnp.dot(inputs, v_weight, preferred_element_type=jnp.float32) + v_bias).astype(
        jnp.bfloat16
    )
    key_rows, value_rows = (
        lax.all_gather(key_part, "mp", axis=0, tiled=True),
        lax.all_gather(value_part, "mp", axis=0, tiled=True),
    )
    visible = lax.iota(jnp.int32, key_rows.shape[0]) < length
    context, log_totals = attend(queries, key_rows, value_rows, visible)
    context_low = context.astype(jnp.bfloat16)
    resid_a = (
        inputs.astype(jnp.float32)
        + jnp.dot(context_low, o_weight, preferred_element_type=jnp.float32)
        + o_bias
    )
    middle, normed_a, inverse_a = norm_forward(resid_a, attn_gain, attn_shift)
    middle_low = middle.astype(jnp.bfloat16)
    pre_act = jnp.dot(middle_low, in_weight, preferred_element_type=jnp.float32) + in_bias
    active_low = jax.nn.gelu(pre_act, approximate=False).astype(jnp.bfloat16)
    resid_f = (
        middle + jnp.dot(active_low, out_weight, preferred_element_type=jnp.float32) + out_bias
    )
    result, normed_f, inverse_f = norm_forward(resid_f, ffn_gain, ffn_shift)
    kept = (
        inputs,
        queries,
        key_rows,
        value_rows,
        visible,
        log_totals,
        context_low,
        normed_a,
        inverse_a,
        middle_low,
        pre_act,
        active_low,
        normed_f,
        inverse_f,
    )
    return (result.astype(jnp.bfloat16), kept)


def backward(whole, kept, cotangent_rows):
    (
        q_weight,
        k_weight,
        v_weight,
        o_weight,
        q_bias,
        v_bias,
        o_bias,
        attn_gain,
        attn_shift,
        in_weight,
        in_bias,
        out_weight,
        out_bias,
        ffn_gain,
        ffn_shift,
    ) = whole
    (
        inputs,
        queries,
        key_rows,
        value_rows,
        visible,
        log_totals,
        context_low,
        normed_a,
        inverse_a,
        middle_low,
        pre_act,
        active_low,
        normed_f,
        inverse_f,
    ) = kept
    grad_final = cotangent_rows.astype(jnp.float32)
    grad_resid_f, grad_gain_f, grad_shift_f = norm_backward(
        grad_final, normed_f, inverse_f, ffn_gain
    )
    grad_branch_f = grad_resid_f.astype(jnp.bfloat16)
    grad_out_bias = jnp.sum(grad_branch_f.astype(jnp.float32), axis=0)
    grad_out_weight = jnp.dot(active_low.T, grad_branch_f, preferred_element_type=jnp.float32)
    grad_active = jnp.dot(grad_branch_f, out_weight.T, preferred_element_type=jnp.float32)
    slope = (
        0.5 * (1.0 + lax.erf(pre_act * root_half))
        + pre_act * jnp.exp(-0.5 * pre_act * pre_act) * inverse_root_two_pi
    )
    grad_pre_low = (grad_active * slope).astype(jnp.bfloat16)
    grad_in_bias = jnp.sum(grad_pre_low.astype(jnp.float32), axis=0)
    grad_in_weight = jnp.dot(middle_low.T, grad_pre_low, preferred_element_type=jnp.float32)
    grad_middle = grad_resid_f + jnp.dot(
        grad_pre_low, in_weight.T, preferred_element_type=jnp.float32
    )
    grad_resid_a, grad_gain_a, grad_shift_a = norm_backward(
        grad_middle, normed_a, inverse_a, attn_gain
    )
    grad_branch_a = grad_resid_a.astype(jnp.bfloat16)
    grad_o_bias = jnp.sum(grad_branch_a.astype(jnp.float32), axis=0)
    grad_o_weight = jnp.dot(context_low.T, grad_branch_a, preferred_element_type=jnp.float32)
    grad_context = jnp.dot(grad_branch_a, o_weight.T, preferred_element_type=jnp.float32).astype(
        jnp.bfloat16
    )
    grad_q, grad_k_part, grad_v_part = attend_back(
        queries, key_rows, value_rows, visible, log_totals, grad_context
    )
    grad_k, grad_v = (
        lax.psum_scatter(
            grad_k_part.astype(jnp.bfloat16), "mp", scatter_dimension=0, tiled=True
        ).astype(jnp.float32),
        lax.psum_scatter(
            grad_v_part.astype(jnp.bfloat16), "mp", scatter_dimension=0, tiled=True
        ).astype(jnp.float32),
    )
    grad_q_low = grad_q.astype(jnp.bfloat16)
    grad_k_low = grad_k.astype(jnp.bfloat16)
    grad_v_low = grad_v.astype(jnp.bfloat16)
    grad_q_bias = jnp.sum(grad_q_low.astype(jnp.float32), axis=0)
    grad_v_bias = jnp.sum(grad_v_low.astype(jnp.float32), axis=0)
    grad_q_weight = jnp.dot(inputs.T, grad_q_low, preferred_element_type=jnp.float32)
    grad_k_weight = jnp.dot(inputs.T, grad_k_low, preferred_element_type=jnp.float32)
    grad_v_weight = jnp.dot(inputs.T, grad_v_low, preferred_element_type=jnp.float32)
    grad_inputs = grad_resid_a + jnp.dot(grad_q_low, q_weight.T, preferred_element_type=jnp.float32)
    grad_inputs = grad_inputs + jnp.dot(grad_k_low, k_weight.T, preferred_element_type=jnp.float32)
    grad_inputs = grad_inputs + jnp.dot(grad_v_low, v_weight.T, preferred_element_type=jnp.float32)
    grads = (
        grad_q_weight,
        grad_k_weight,
        grad_v_weight,
        grad_o_weight,
        grad_q_bias,
        grad_v_bias,
        grad_o_bias,
        grad_gain_a,
        grad_shift_a,
        grad_in_weight,
        grad_in_bias,
        grad_out_weight,
        grad_out_bias,
        grad_gain_f,
        grad_shift_f,
    )
    return (grads, grad_inputs)


def on_device(
    tokens,
    lengths,
    order,
    q_weight,
    k_weight,
    v_weight,
    o_weight,
    q_bias,
    v_bias,
    o_bias,
    attn_gain,
    attn_shift,
    in_weight,
    in_bias,
    out_weight,
    out_bias,
    ffn_gain,
    ffn_shift,
    cotangent,
):

    def settle(running, grads):
        if running is None:
            return tuple(grads)
        return tuple((first + second for first, second in zip(running, grads)))

    micro_count = tokens.shape[0]
    dealt = deal_rows(tokens, order)
    live_all = jnp.take(lengths, order, axis=0)
    live_mine = lax.dynamic_slice_in_dim(
        live_all, lax.axis_index("dp") * micro_count, micro_count, 0
    )
    results = []
    input_grads = []
    running = None
    kept_all = []
    for micro in range(micro_count):
        whole = (
            lax.all_gather(q_weight, ("dp", "mp"), axis=0, tiled=True),
            lax.all_gather(k_weight, ("dp", "mp"), axis=0, tiled=True),
            lax.all_gather(v_weight, ("dp", "mp"), axis=0, tiled=True),
            lax.all_gather(o_weight, ("dp", "mp"), axis=0, tiled=True),
            lax.all_gather(q_bias, ("dp", "mp"), axis=0, tiled=True),
            lax.all_gather(v_bias, ("dp", "mp"), axis=0, tiled=True),
            lax.all_gather(o_bias, ("dp", "mp"), axis=0, tiled=True),
            lax.all_gather(attn_gain, ("dp", "mp"), axis=0, tiled=True),
            lax.all_gather(attn_shift, ("dp", "mp"), axis=0, tiled=True),
            lax.all_gather(in_weight, ("dp", "mp"), axis=0, tiled=True),
            lax.all_gather(in_bias, ("dp", "mp"), axis=0, tiled=True),
            lax.all_gather(out_weight, ("dp", "mp"), axis=0, tiled=True),
            lax.all_gather(out_bias, ("dp", "mp"), axis=0, tiled=True),
            lax.all_gather(ffn_gain, ("dp", "mp"), axis=0, tiled=True),
            lax.all_gather(ffn_shift, ("dp", "mp"), axis=0, tiled=True),
        )
        result, kept = forward(whole, dealt[micro], live_mine[micro])
        kept_all.append(kept)
        results.append(result)
    for micro in range(micro_count):
        whole = (
            lax.all_gather(q_weight, ("dp", "mp"), axis=0, tiled=True),
            lax.all_gather(k_weight, ("dp", "mp"), axis=0, tiled=True),
            lax.all_gather(v_weight, ("dp", "mp"), axis=0, tiled=True),
            lax.all_gather(o_weight, ("dp", "mp"), axis=0, tiled=True),
            lax.all_gather(q_bias, ("dp", "mp"), axis=0, tiled=True),
            lax.all_gather(v_bias, ("dp", "mp"), axis=0, tiled=True),
            lax.all_gather(o_bias, ("dp", "mp"), axis=0, tiled=True),
            lax.all_gather(attn_gain, ("dp", "mp"), axis=0, tiled=True),
            lax.all_gather(attn_shift, ("dp", "mp"), axis=0, tiled=True),
            lax.all_gather(in_weight, ("dp", "mp"), axis=0, tiled=True),
            lax.all_gather(in_bias, ("dp", "mp"), axis=0, tiled=True),
            lax.all_gather(out_weight, ("dp", "mp"), axis=0, tiled=True),
            lax.all_gather(out_bias, ("dp", "mp"), axis=0, tiled=True),
            lax.all_gather(ffn_gain, ("dp", "mp"), axis=0, tiled=True),
            lax.all_gather(ffn_shift, ("dp", "mp"), axis=0, tiled=True),
        )
        grads, grad_inputs = backward(whole, kept_all[micro], cotangent[micro])
        running = settle(running, grads)
        input_grads.append(grad_inputs)
    owned = (
        lax.psum_scatter(running[0], ("dp", "mp"), scatter_dimension=0, tiled=True),
        lax.psum_scatter(running[1], ("dp", "mp"), scatter_dimension=0, tiled=True),
        lax.psum_scatter(running[2], ("dp", "mp"), scatter_dimension=0, tiled=True),
        lax.psum_scatter(running[3], ("dp", "mp"), scatter_dimension=0, tiled=True),
        lax.psum_scatter(running[4], ("dp", "mp"), scatter_dimension=0, tiled=True),
        lax.psum_scatter(running[5], ("dp", "mp"), scatter_dimension=0, tiled=True),
        lax.psum_scatter(running[6], ("dp", "mp"), scatter_dimension=0, tiled=True),
        lax.psum_scatter(running[7], ("dp", "mp"), scatter_dimension=0, tiled=True),
        lax.psum_scatter(running[8], ("dp", "mp"), scatter_dimension=0, tiled=True),
        lax.psum_scatter(running[9], ("dp", "mp"), scatter_dimension=0, tiled=True),
        lax.psum_scatter(running[10], ("dp", "mp"), scatter_dimension=0, tiled=True),
        lax.psum_scatter(running[11], ("dp", "mp"), scatter_dimension=0, tiled=True),
        lax.psum_scatter(running[12], ("dp", "mp"), scatter_dimension=0, tiled=True),
        lax.psum_scatter(running[13], ("dp", "mp"), scatter_dimension=0, tiled=True),
        lax.psum_scatter(running[14], ("dp", "mp"), scatter_dimension=0, tiled=True),
    )
    return (jnp.stack(results), jnp.stack(input_grads)) + tuple(owned)


def solution(mesh):
    placed = (
        P("dp", "mp", None),
        P(),
        P(),
        P(("dp", "mp"), None),
        P(("dp", "mp"), None),
        P(("dp", "mp"), None),
        P(("dp", "mp"), None),
        P(("dp", "mp")),
        P(("dp", "mp")),
        P(("dp", "mp")),
        P(("dp", "mp")),
        P(("dp", "mp")),
        P(("dp", "mp"), None),
        P(("dp", "mp")),
        P(("dp", "mp"), None),
        P(("dp", "mp")),
        P(("dp", "mp")),
        P(("dp", "mp")),
        P("dp", "mp", None),
    )
    return jax.shard_map(
        on_device,
        mesh=mesh,
        in_specs=placed,
        out_specs=(
            P("dp", "mp", None),
            P("dp", "mp", None),
            P(("dp", "mp"), None),
            P(("dp", "mp"), None),
            P(("dp", "mp"), None),
            P(("dp", "mp"), None),
            P(("dp", "mp")),
            P(("dp", "mp")),
            P(("dp", "mp")),
            P(("dp", "mp")),
            P(("dp", "mp")),
            P(("dp", "mp"), None),
            P(("dp", "mp")),
            P(("dp", "mp"), None),
            P(("dp", "mp")),
            P(("dp", "mp")),
            P(("dp", "mp")),
        ),
        check_vma=False,
    )
```

profile of v0, /device:TPU:0, one launch (start us, length us, event | category | flops | bytes accessed | tf_op | source)
XLA Modules:
  0.0 1737.8 jit_solution(16937414632751804318)
XLA Ops:
  10.6 7.3 all-to-all-start
  20.0 37.1 %all-to-all-done = bf16[2,8,64,768]{3,2,0,1:T(8,128)(2,1)S(1)} async-done(((bf16[2,8,64,768]{3,2,0,1:T(8,128)(2,1)}), bf16[2,8,64,768]{3,2,0,1:T(8,128)(2,1)S(1)}, u32[]{:S(2)}, u32[]{:S(2)}) %all-to-all-start) | async-done | bytes 1572896 | tf_op jit(solution)/shard_map/all_to_all | solution.py:98
  59.2 3.7 all-to-all-start.1
  65.9 57.7 %all-reduce.19 = (bf16[768]{0:T(1024)(128)(2,1)}, bf16[768]{0:T(1024)(128)(2,1)S(1)}, bf16[768]{0:T(1024)(128)(2,1)}, bf16[768]{0:T(1024)(128)(2,1)}, bf16[768]{...) all-reduce(bf16[768]{0:T(1024)(128)(2,1)S(1)} %dynamic-update-slice, ...), channel_id=1, replica_groups=mesh['dp'=8,'mp'=4] {'dp','mp'}, use_global_device_ids=true, to_apply=%add | all-reduce | flops 9216 | bytes 36864
  129.8 16.8 all-gather.13.cloned.1.call-done
  159.1 43.4 %all-gather.11.cloned.1.call-done = bf16[768,768]{1,0:T(8,128)(2,1)} async-done(((bf16[24,768]{1,0:T(8,128)(2,1)}), bf16[768,768]{1,0:T(8,128)(2,1)}) %all-gather.11.cloned.1.call-update) | async-done | bytes 1179664 | tf_op jit(solution)/shard_map/all_gather | solution.py:312
  210.3 21.7 %all-gather.19.cloned.1.call-done = bf16[2048,768]{1,0:T(8,128)(2,1)} async-done(((bf16[512,768]{1,0:T(8,128)(2,1)}), bf16[2048,768]{1,0:T(8,128)(2,1)}) %all-gather.19.cloned.1.call-update) | async-done | bytes 3145744 | tf_op jit(solution)/shard_map/all_gather | solution.py:133
  232.0 4.6 copy.93
  236.7 6.7 copy.96
  243.4 18.6 %all-gather.15.cloned.1.call-done = bf16[2048,768]{1,0:T(8,128)(2,1)} async-done(((bf16[512,768]{1,0:T(8,128)(2,1)}), bf16[2048,768]{1,0:T(8,128)(2,1)}) %all-gather.15.cloned.1.call-update) | async-done | bytes 3145744 | tf_op jit(solution)/shard_map/all_gather | solution.py:132
  262.0 4.6 copy.92
  266.6 6.6 copy.95
  273.3 109.9 %while.56 = (s32[]{:T(128)}, bf16[12,512,64]{1,2,0:T(8,128)(2,1)S(1)}, f32[12,512]{1,0:T(8,128)S(1)}, bf16[12,512,64]{2,1,0:T(8,128)(2,1)}, bf16[12,2048,64]{2,1...) while((s32[]{:T(128)}, ...), condition=%wide.region_3.4_spmd.clone, body=%wide.region_0.3_spmd.clone.sunk | while | flops 281019904 | bytes 30701696 | solution.py:58
  324.5 3.9 fusion.277
  386.8 4.6 copy.99
  391.5 6.6 copy.102
  398.1 4.6 copy.98
  402.7 6.6 copy.101
  409.4 111.7 %while.57 = (s32[]{:T(128)}, bf16[12,512,64]{1,2,0:T(8,128)(2,1)S(1)}, f32[12,512]{1,0:T(8,128)S(1)}, bf16[12,512,64]{2,1,0:T(8,128)(2,1)}, bf16[12,2048,64]{2,1...) while((s32[]{:T(128)}, ...), condition=%wide.region_11.12_spmd.clone, body=%wide.region_8.11_spmd.clone.sunk | while | flops 281019904 | bytes 30701696 | solution.py:58
  424.2 4.2 fusion.281
  489.1 4.2 fusion.281
  508.1 3.7 fusion.281
  524.8 4.9 fusion.157
  532.4 31.6 %fusion.94 = (bf16[512,3072]{1,0:T(8,128)(2,1)}, bf16[512,3072]{1,0:T(8,128)(2,1)}, f32[512,3072]{1,0:T(8,128)}) fusion(f32[3072]{0:T(1024)S(1)} %convert_element_type.267, f32[512,3072]{1,0:T(8,128)S(1)} %fusion.157, bf16[768,3072]{1,0:T(8,128)(2,1)S(1)} %copy-done.59, f32[512,768]{1,0:T(8,128)S(1)} %copy-done.29, f32[768]{0:T(1024)S(1)} %convert_element_type.265, ...), kind=kOutput, calls=%fused_computation.122 | convolution fusion | flops 2625503232 | bytes 25188352 | tf_op jit(solution)/shard_map/dot_general | solution.py:145
  564.1 6.2 fusion.170
  579.0 8.2 convert_reduce_fusion.1
  587.3 3.6 multiply_reduce_fusion.3
  590.9 5.3 convert_reduce_fusion
  596.3 5.4 convert_reduce_fusion.7
  608.2 136.0 %while.58 = (s32[]{:T(128)}, bf16[12,512,64]{1,2,0:T(8,128)(2,1)S(1)}, bf16[12,2048,64]{1,2,0:T(8,128)(2,1)}, bf16[12,2048,64]{1,2,0:T(8,128)(2,1)}, bf16[12,512...) while((s32[]{:T(128)}, ...), condition=%wide.region_22.23_spmd.clone, body=%wide.region_20.22_spmd.clone.sunk | while | flops 680691200 | bytes 34622580 | solution.py:80
  756.5 153.9 %while.59 = (s32[]{:T(128)}, bf16[12,512,64]{1,2,0:T(8,128)(2,1)}, bf16[12,2048,64]{1,2,0:T(8,128)(2,1)}, bf16[12,2048,64]{1,2,0:T(8,128)(2,1)}, bf16[12,512,64]...) while((s32[]{:T(128)}, bf16[12,512,64]{1,2,0:T(8,128)(2,1)}, ...), condition=%wide.region_31.32_spmd.clone, body=%wide.region_29.31_spmd.clone.sunk | while | flops 680691200 | bytes 34622580 | solution.py:80
  926.3 22.0 %reduce-scatter.17.cloned.1.call-done = bf16[512,768]{0,1:T(8,128)(2,1)} async-done(((bf16[2048,768]{0,1:T(8,128)(2,1)}), bf16[512,768]{0,1:T(8,128)(2,1)}) %reduce-scatter.17.cloned.1.call-update) | async-done | bytes 786448 | tf_op jit(solution)/shard_map/reduce_scatter | solution.py:238
  948.2 4.4 convolution_add_fusion.3
  952.7 36.1 %reduce-scatter.11.cloned.1.call-done = bf16[512,768]{0,1:T(8,128)(2,1)} async-done(((bf16[2048,768]{0,1:T(8,128)(2,1)}), bf16[512,768]{0,1:T(8,128)(2,1)}) %reduce-scatter.11.cloned.1.call-update) | async-done | bytes 786448 | tf_op jit(solution)/shard_map/reduce_scatter | solution.py:235
  988.8 3.7 fusion.176
  992.5 36.8 %reduce-scatter.15.cloned.1.call-done = bf16[512,768]{0,1:T(8,128)(2,1)} async-done(((bf16[2048,768]{0,1:T(8,128)(2,1)}), bf16[512,768]{0,1:T(8,128)(2,1)}) %reduce-scatter.15.cloned.1.call-update) | async-done | bytes 786448 | tf_op jit(solution)/shard_map/reduce_scatter | solution.py:235
  1029.3 4.5 convolution_add_fusion.4
  1034.2 5.2 fusion.153
  1039.4 5.4 convolution_add_fusion
  1045.5 5.5 fusion.159
  1051.0 5.7 convolution_add_fusion.1
  1069.7 40.8 %all-reduce.18 = (f32[768]{0:T(1024)S(1)}, f32[768]{0:T(1024)S(1)}, f32[768]{0:T(1024)S(1)}, f32[768]{0:T(1024)S(1)}, f32[768]{0:T(1024)S(1)}, /*index=5*/f32[30...) all-reduce(f32[768]{0:T(1024)S(1)} %add.363, ...), channel_id=10, replica_groups=mesh['dp'=8,'mp'=4] {'dp','mp'}, use_global_device_ids=true, to_apply=%region_40.41.clone | all-reduce | flops 9216 | bytes 73728
  1123.4 10.9 reduce-scatter.25.cloned.1.call-done
  1134.3 104.6 %reduce-scatter.19.cloned.1.call-done = f32[24,768]{1,0:T(8,128)} async-done(((f32[768,768]{1,0:T(8,128)}), f32[24,768]{1,0:T(8,128)}) %reduce-scatter.19.cloned.1.call-update) | async-done | bytes 73744 | tf_op jit(solution)/shard_map/reduce_scatter | solution.py:353
  1238.8 103.8 %reduce-scatter.23.cloned.1.call-done = f32[24,768]{1,0:T(8,128)} async-done(((f32[768,768]{1,0:T(8,128)}), f32[24,768]{1,0:T(8,128)}) %reduce-scatter.23.cloned.1.call-update) | async-done | bytes 73744 | tf_op jit(solution)/shard_map/reduce_scatter | solution.py:355
  1342.7 104.6 %reduce-scatter.21.cloned.1.call-done = f32[24,768]{1,0:T(8,128)} async-done(((f32[768,768]{1,0:T(8,128)}), f32[24,768]{1,0:T(8,128)}) %reduce-scatter.21.cloned.1.call-update) | async-done | bytes 73744 | tf_op jit(solution)/shard_map/reduce_scatter | solution.py:354
  1447.2 141.2 %reduce-scatter.29.cloned.1.call-done = f32[96,768]{1,0:T(8,128)} async-done(((f32[3072,768]{1,0:T(8,128)}), f32[96,768]{1,0:T(8,128)}) %reduce-scatter.29.cloned.1.call-update) | async-done | bytes 294928 | tf_op jit(solution)/shard_map/reduce_scatter | solution.py:364
  1588.4 142.0 %reduce-scatter.27.cloned.1.call-done = f32[24,3072]{1,0:T(8,128)} async-done(((f32[768,3072]{1,0:T(8,128)}), f32[24,3072]{1,0:T(8,128)}) %reduce-scatter.27.cloned.1.call-update) | async-done | bytes 294928 | tf_op jit(solution)/shard_map/reduce_scatter | solution.py:362
  (709 shorter events, 609.8 us)
Async XLA Ops:
  7.2 11.5 copy-start
  7.2 119.1 %all-gather.17.cloned.1.call-start = ((), (), s32[]{:S(2)}) async-start(), calls=%async_computation.15 | async-start | bytes 1216512 | tf_op jit(solution)/shard_map/all_gather | solution.py:314
  7.9 10.7 copy-start.57
  10.6 46.4 %all-to-all-start = ((bf16[2,8,64,768]{3,2,0,1:T(8,128)(2,1)}), bf16[2,8,64,768]{3,2,0,1:T(8,128)(2,1)S(1)}, u32[]{:S(2)}, u32[]{:S(2)}) async-start(bf16[2,8,64,768]{3,2,0,1:T(8,128)(2,1)} %copy.90), calls=%async_computation | async-start | bytes 3145728 | tf_op jit(solution)/shard_map/all_to_all | solution.py:98
  17.9 128.7 %all-gather.13.cloned.1.call-start = ((), (), s32[]{:S(2)}) async-start(), calls=%async_computation.13 | async-start | bytes 1216512 | tf_op jit(solution)/shard_map/all_gather | solution.py:313
  57.8 6.7 copy-start.68
  57.8 6.9 copy-start.69
  57.8 7.1 copy-start.70
  57.8 7.3 copy-start.71
  57.8 7.5 copy-start.72
  57.8 7.8 copy-start.73
  59.2 64.4 %all-to-all-start.1 = ((bf16[8,2,64,768]{3,2,1,0:T(8,128)(2,1)}), bf16[8,2,64,768]{3,2,1,0:T(8,128)(2,1)S(1)}, u32[]{:S(2)}, u32[]{:S(2)}) async-start(bf16[8,2,64,768]{3,2,1,0:T(8,128)(2,1)} %broadcast_select_fusion), calls=%async_computation.1 | async-start | bytes 3145728 | tf_op jit(solution)/shard_map/all_to_all | solution.py:102
  62.9 139.6 %all-gather.11.cloned.1.call-start = ((), (), s32[]{:S(2)}) async-start(), calls=%async_computation.12 | async-start | bytes 1216512 | tf_op jit(solution)/shard_map/all_gather | solution.py:312
  63.6 168.4 %all-gather.19.cloned.1.call-start = ((), (), s32[]{:S(2)}) async-start(), calls=%async_computation.16 | async-start | bytes 3932160 | tf_op jit(solution)/shard_map/all_gather | solution.py:133
  126.2 257.0 %copy-start.8 = (bf16[1,1,8,64,768]{4,3,1,2,0:T(8,128)(2,1)}, bf16[1,1,8,64,768]{4,3,1,2,0:T(8,128)(2,1)S(1)}, u32[]{:S(2)}) copy-start(bf16[1,1,8,64,768]{4,3,1,2,0:T(8,128)(2,1)S(1)} %get-tuple-element.520) | copy-start | bytes 2359300
  126.3 395.5 %copy-start.6 = (bf16[1,1,8,64,768]{4,3,1,2,0:T(8,128)(2,1)}, bf16[1,1,8,64,768]{4,3,1,2,0:T(8,128)(2,1)S(1)}, u32[]{:S(2)}) copy-start(bf16[1,1,8,64,768]{4,3,1,2,0:T(8,128)(2,1)S(1)} %get-tuple-element.521) | copy-start | bytes 2359300
  129.8 20.5 %copy-start.20 = (bf16[768,768]{1,0:T(8,128)(2,1)S(1)}, bf16[768,768]{1,0:T(8,128)(2,1)}, u32[]{:S(2)}) copy-start(bf16[768,768]{1,0:T(8,128)(2,1)} %all-gather.17.cloned.1.call-done) | copy-start | bytes 3538948
  129.8 132.2 %all-gather.15.cloned.1.call-start = ((), (), s32[]{:S(2)}) async-start(), calls=%async_computation.14 | async-start | bytes 3932160 | tf_op jit(solution)/shard_map/all_gather | solution.py:132
  149.6 233.6 %all-gather.21.cloned.1.call-start = ((), (), s32[]{:S(2)}) async-start(), calls=%async_computation.17 | async-start | bytes 1216512 | tf_op jit(solution)/shard_map/all_gather | solution.py:315
  150.2 236.6 %all-gather.29.cloned.1.call-start = ((), (), s32[]{:S(2)}) async-start(), calls=%async_computation.21 | async-start | bytes 3932160 | tf_op jit(solution)/shard_map/all_gather | solution.py:133
  152.0 246.1 %all-gather.27.cloned.1.call-start = ((), (), s32[]{:S(2)}) async-start(), calls=%async_computation.20 | async-start | bytes 3932160 | tf_op jit(solution)/shard_map/all_gather | solution.py:132
  155.0 369.8 %all-gather.23.cloned.1.call-start = ((), (), s32[]{:S(2)}) async-start(), calls=%async_computation.18 | async-start | bytes 4866048 | tf_op jit(solution)/shard_map/all_gather | solution.py:321
  155.8 408.3 %all-gather.25.cloned.1.call-start = ((), (), s32[]{:S(2)}) async-start(), calls=%async_computation.19 | async-start | bytes 4866048 | tf_op jit(solution)/shard_map/all_gather | solution.py:323
  156.4 766.3 %reduce-scatter.13.cloned.1.call-start = ((), (), s32[]{:S(2)}) async-start(), calls=%async_computation.23 | async-start | bytes 3932160 | tf_op jit(solution)/shard_map/reduce_scatter | solution.py:238
  157.3 413.3 %copy-start.33 = (f32[768]{0:T(1024)}, f32[768]{0:T(1024)S(1)}, u32[]{:S(2)}) copy-start(f32[768]{0:T(1024)S(1)} %convert_element_type.265) | copy-start | bytes 9220
  383.2 8.2 copy-start.25
  383.2 8.2 copy-start.35
  524.8 7.7 copy-start.29
  524.8 7.6 copy-start.59
  532.4 31.6 %copy-start.50 = (f32[768]{0:T(1024)S(1)}, f32[768]{0:T(1024)}, u32[]{:S(2)}) copy-start(f32[768]{0:T(1024)} %convert_element_type.269) | copy-start | bytes 9220
  576.0 11.2 slice-start
  576.1 14.9 slice-start.2
  579.0 8.2 copy-start.16
  579.0 17.3 copy-start.14
  579.0 8.2 slice-start.1
  579.0 11.9 slice-start.3
  744.3 203.9 %reduce-scatter.17.cloned.1.call-start = ((), (), s32[]{:S(2)}) async-start(), calls=%async_computation.25 | async-start | bytes 3932160 | tf_op jit(solution)/shard_map/reduce_scatter | solution.py:238
  910.4 78.3 %reduce-scatter.11.cloned.1.call-start = ((), (), s32[]{:S(2)}) async-start(), calls=%async_computation.22 | async-start | bytes 3932160 | tf_op jit(solution)/shard_map/reduce_scatter | solution.py:235
  911.2 118.2 %reduce-scatter.15.cloned.1.call-start = ((), (), s32[]{:S(2)}) async-start(), calls=%async_computation.24 | async-start | bytes 3932160 | tf_op jit(solution)/shard_map/reduce_scatter | solution.py:235
  911.7 222.5 %reduce-scatter.25.cloned.1.call-start = ((), (), s32[]{:S(2)}) async-start(), calls=%async_computation.29 | async-start | bytes 2433024 | tf_op jit(solution)/shard_map/reduce_scatter | solution.py:356
  916.6 322.3 %reduce-scatter.19.cloned.1.call-start = ((), (), s32[]{:S(2)}) async-start(), calls=%async_computation.26 | async-start | bytes 2433024 | tf_op jit(solution)/shard_map/reduce_scatter | solution.py:353
  922.6 420.1 %reduce-scatter.23.cloned.1.call-start = ((), (), s32[]{:S(2)}) async-start(), calls=%async_computation.28 | async-start | bytes 2433024 | tf_op jit(solution)/shard_map/reduce_scatter | solution.py:355
  952.7 494.6 %reduce-scatter.21.cloned.1.call-start = ((), (), s32[]{:S(2)}) async-start(), calls=%async_computation.27 | async-start | bytes 2433024 | tf_op jit(solution)/shard_map/reduce_scatter | solution.py:354
  1033.9 554.6 %reduce-scatter.29.cloned.1.call-start = ((), (), s32[]{:S(2)}) async-start(), calls=%async_computation.31 | async-start | bytes 9732096 | tf_op jit(solution)/shard_map/reduce_scatter | solution.py:364
  1044.8 685.6 %reduce-scatter.27.cloned.1.call-start = ((), (), s32[]{:S(2)}) async-start(), calls=%async_computation.30 | async-start | bytes 9732096 | tf_op jit(solution)/shard_map/reduce_scatter | solution.py:362
  1110.6 7.8 copy-start.32
  1110.6 7.8 copy-start.61
  1120.6 609.8 %copy-start.1 = (s32[16]{0:T(128)S(1)}, s32[16]{0:T(128)}, u32[]{:S(2)}) copy-start(s32[16]{0:T(128)} %param.28) | copy-start | bytes 196
  (76 other events, 256.4 us)
Sparse Core Ops, SparseCore 0:
  10.9 70.6 all-gather.16
  84.6 62.0 all-gather.12
  149.5 52.9 all-gather.10
  204.5 27.4 all-gather.18
  233.4 28.5 all-gather.14
  264.8 54.0 all-gather.20
  320.4 27.5 all-gather.28
  349.5 28.5 all-gather.26
  381.0 63.6 all-gather.22
  447.4 62.4 all-gather.24
  744.4 37.7 reduce-scatter.12
  910.5 37.6 reduce-scatter.16
  950.8 37.9 reduce-scatter.10
  991.3 37.9 reduce-scatter.14
  1035.0 99.2 reduce-scatter.24
  1140.9 97.9 reduce-scatter.18
  1244.5 98.0 reduce-scatter.22
  1349.2 97.9 reduce-scatter.20
  1453.7 134.6 reduce-scatter.28
  1595.7 134.6 reduce-scatter.26
where the time goes:
time: 1750 us; the launch traced here: 1740 us
  waiting for transfers between devices  845 us (48%)
  matrix products  530 us (30%)
  local copies, waits for them, and re-layouts  150 us (9%)
  blocking collectives  98.6 us (6%)
  other arithmetic  84.4 us (5%)
    reduce_scatter x1, waiting for transfers between devices, on_device(): lax.psum_scatter(running[9], ('dp', 'mp'), scatter_dimension=0, tiled=True)  142 us
    reduce_scatter x1, waiting for transfers between devices, on_device(): lax.psum_scatter(running[11], ('dp', 'mp'), scatter_dimension=0, tiled=True)  141 us
    dot_general x48, matrix products, head_scores(): jnp.einsum('qd,kd->qk', head_q, head_k, preferred_element_type=jnp.float32)  108 us
    reduce_scatter x1, waiting for transfers between devices, on_device(): lax.psum_scatter(running[0], ('dp', 'mp'), scatter_dimension=0, tiled=True)  105 us
    reduce_scatter x1, waiting for transfers between devices, on_device(): lax.psum_scatter(running[1], ('dp', 'mp'), scatter_dimension=0, tiled=True)  105 us
    reduce_scatter x1, waiting for transfers between devices, on_device(): lax.psum_scatter(running[2], ('dp', 'mp'), scatter_dimension=0, tiled=True)  104 us
    unnamed x2, blocking collectives  98.6 us
    dot_general x24, matrix products, per_head(): context = jnp.dot(shares, head_v, preferred_element_type=jnp.float32)  86.6 us
  transfers between devices with their start and end apart: 22, of which 14 were waited for; matrix products, arithmetic and copies ran while one was open for 30% of the time, Pallas kernels for 0%

commit v1 on v0

v1 whole, which is shorter than its diff:
```python
import functools
import jax, jax.numpy as jnp
from jax import lax
from jax.experimental import pallas as pl
from jax.experimental.pallas import tpu as pltpu
bf=jnp.bfloat16; f32=jnp.float32
HD=64
NEG=-1e30

def _assemble(own_ref, sib_ref, full_ref, c, x, piece):
    rows=own_ref.shape[0]
    for b in range(rows//piece):
        y=x if b==0 else 1-x
        full_ref[pl.ds((2*y+c)*piece,piece),:]=own_ref[b*piece:(b+1)*piece,:]
        full_ref[pl.ds((2*y+1-c)*piece,piece),:]=sib_ref[b*piece:(b+1)*piece,:]

def _masked_rows(t):
    row=lax.broadcasted_iota(jnp.int32,t.shape,0)
    z=jnp.zeros_like(t)
    return jnp.where(row<HD,t,z), jnp.where(row<HD,z,t)
def _masked_lanes(t):
    col=lax.broadcasted_iota(jnp.int32,t.shape,1)
    z=jnp.zeros_like(t)
    return jnp.where(col<HD,t,z), jnp.where(col<HD,z,t)

def dot(a,b): return jnp.dot(a,b,preferred_element_type=f32)

def fwd_kernel(piece, KB, QB, live_ref, q_ref, ko_ref, vo_ref, ks_ref, vs_ref, c_ref, lse_ref,
               kfull, vfull, vT0, vT1, qT0, qT1, acc):
    live=live_ref[0]; c=live_ref[1]; x=live_ref[2]
    _assemble(ko_ref,ks_ref,kfull,c,x,piece)
    _assemble(vo_ref,vs_ref,vfull,c,x,piece)
    L=kfull.shape[0]; nq=q_ref.shape[0]
    for i in range(0,L,512):
        t=jnp.transpose(vfull[i:i+512,:])
        a,b=_masked_rows(t); vT0[:,i:i+512]=a; vT1[:,i:i+512]=b
    for i in range(0,nq,512):
        t=jnp.transpose(q_ref[i:i+512,:]*jnp.asarray(0.125,bf))
        a,b=_masked_rows(t); qT0[:,i:i+512]=a; qT1[:,i:i+512]=b
    nb=(live+KB-1)//KB
    rowsel=lax.broadcasted_iota(jnp.int32,(2*HD,QB),0)<HD
    for qi in range(nq//QB):
        qs=slice(qi*QB,(qi+1)*QB)
        acc[...]=jnp.zeros_like(acc)
        def block(j,carry,masked):
            m0,l0,m1,l1=carry
            ks=pl.multiple_of(j*KB,KB)
            kb=kfull[pl.ds(ks,KB),:]
            s0=dot(kb,qT0[:,qs]); s1=dot(kb,qT1[:,qs])
            if masked:
                keep=lax.broadcasted_iota(jnp.int32,(KB,QB),0)+ks<live
                s0=jnp.where(keep,s0,NEG); s1=jnp.where(keep,s1,NEG)
            n0=jnp.maximum(m0,jnp.max(s0,axis=0,keepdims=True)); n1=jnp.maximum(m1,jnp.max(s1,axis=0,keepdims=True))
            p0=jnp.exp(s0-n0); p1=jnp.exp(s1-n1)
            a0=jnp.exp(m0-n0); a1=jnp.exp(m1-n1)
            l0=l0*a0+jnp.sum(p0,axis=0,keepdims=True); l1=l1*a1+jnp.sum(p1,axis=0,keepdims=True)
            pv=dot(vT0[:,pl.ds(ks,KB)],p0.astype(bf))+dot(vT1[:,pl.ds(ks,KB)],p1.astype(bf))
            acc[...]=acc[...]*jnp.where(rowsel,a0,a1)+pv
            return n0,l0,n1,l1
        init=(jnp.full((1,QB),NEG,f32),jnp.zeros((1,QB),f32))*2
        carry=lax.fori_loop(0,nb-1,lambda j,cr:block(j,cr,False),init)
        m0,l0,m1,l1=block(nb-1,carry,True)
        o=acc[...]*jnp.where(rowsel,1.0/l0,1.0/l1)
        c_ref[qs,:]=jnp.transpose(o).astype(bf)
        lse_ref[0,0:1,qs]=m0+jnp.log(l0); lse_ref[0,1:2,qs]=m1+jnp.log(l1)

def attn_fwd(q, kvo, kvs, sc, piece, KB=256, QB=1024):
    nq,w=q.shape; pairs=w//128; L=2*kvo.shape[0]
    qspec=lambda off: pl.BlockSpec((nq,128),lambda p,s:(0,p+off))
    kspec=lambda off: pl.BlockSpec((L//2,128),lambda p,s:(0,p+off))
    return pl.pallas_call(functools.partial(fwd_kernel,piece,KB,QB),
        grid_spec=pltpu.PrefetchScalarGridSpec(num_scalar_prefetch=1,grid=(pairs,),
            in_specs=[qspec(0),kspec(0),kspec(pairs),kspec(0),kspec(pairs)],
            out_specs=[qspec(0),pl.BlockSpec((1,2,nq),lambda p,s:(p,0,0))],
            scratch_shapes=[pltpu.VMEM((L,128),bf)]*2+[pltpu.VMEM((128,L),bf)]*2+[pltpu.VMEM((128,nq),bf)]*2+[pltpu.VMEM((128,QB),f32)]),
        out_shape=(jax.ShapeDtypeStruct((nq,w),bf),jax.ShapeDtypeStruct((pairs,2,nq),f32)),
        name="attn_fwd",
        cost_estimate=pl.CostEstimate(flops=int(4*nq*L*w*0.6*3),bytes_accessed=6*nq*w*2*2,transcendentals=int(nq*L*w/64*0.6)),
        compiler_params=pltpu.CompilerParams(vmem_limit_bytes=40*2**20,dimension_semantics=("arbitrary",)))(sc,q,kvo,kvo,kvs,kvs)

def bwd_kernel(piece, KB, QB, live_ref, q_ref, ko_ref, vo_ref, ks_ref, vs_ref, c_ref, dc_ref, lse_ref, dq_ref, dko_ref, dvo_ref, dks_ref, dvs_ref,
               kfull, vfull, kT0, kT1, qT0, qT1, dT0, dT1, qm0,qm1,dm0,dm1, delta, dkf, dvf, dqT):
    live=live_ref[0]; c=live_ref[1]; x=live_ref[2]
    _assemble(ko_ref,ks_ref,kfull,c,x,piece)
    _assemble(vo_ref,vs_ref,vfull,c,x,piece)
    L=kfull.shape[0]; nq=q_ref.shape[0]
    for i in range(0,L,512):
        t=jnp.transpose(kfull[i:i+512,:])
        a,b=_masked_rows(t); kT0[:,i:i+512]=a; kT1[:,i:i+512]=b
    for i in range(0,nq,512):
        s=slice(i,i+512)
        qf=q_ref[s,:]*jnp.asarray(0.125,bf)
        a,b=_masked_rows(jnp.transpose(qf)); qT0[:,s]=a; qT1[:,s]=b
        a,b=_masked_lanes(qf); qm0[s,:]=a; qm1[s,:]=b
        d=dc_ref[s,:]; df=d.astype(f32)
        dt=jnp.transpose(d)
        a,b=_masked_rows(dt); dT0[:,s]=a; dT1[:,s]=b
        a,b=_masked_lanes(d); dm0[s,:]=a; dm1[s,:]=b
        prod=jnp.transpose(df*c_ref[s,:].astype(f32))
        delta[0:1,s]=jnp.sum(prod[:HD],axis=0,keepdims=True); delta[1:2,s]=jnp.sum(prod[HD:],axis=0,keepdims=True)
    dqT[...]=jnp.zeros_like(dqT)
    nb=(live+KB-1)//KB
    def zero(j,_):
        ks=pl.multiple_of(j*KB,KB)
        dkf[pl.ds(ks,KB),:]=jnp.zeros((KB,128),bf); dvf[pl.ds(ks,KB),:]=jnp.zeros((KB,128),bf)
        return 0
    lax.fori_loop(nb,L//KB,zero,0)
    def block(j,masked):
        ks=pl.multiple_of(j*KB,KB)
        kb=kfull[pl.ds(ks,KB),:]; vb=vfull[pl.ds(ks,KB),:]
        k0=kT0[:,pl.ds(ks,KB)]; k1=kT1[:,pl.ds(ks,KB)]
        dk=None; dv=None
        for qi in range(nq//QB):
            qs=slice(qi*QB,(qi+1)*QB)
            dq=None
            for qT,dT,qm,dm,kT,h in ((qT0,dT0,qm0,dm0,k0,0),(qT1,dT1,qm1,dm1,k1,1)):
                s=dot(kb,qT[:,qs])
                p=jnp.exp(s-lse_ref[0,h:h+1,qs])
                if masked:
                    keep=lax.broadcasted_iota(jnp.int32,(KB,QB),0)+ks<live
                    p=jnp.where(keep,p,0.0)
                dp=dot(vb,dT[:,qs])
                ds=(p*(dp-delta[h:h+1,qs])).astype(bf)
                v_=dot(p.astype(bf),dm[qs,:]); k_=dot(ds,qm[qs,:]); q_=dot(kT,ds)
                dv=v_ if dv is None else dv+v_
                dk=k_ if dk is None else dk+k_
                dq=q_ if dq is None else dq+q_
            dqT[:,qs]+=dq
        dkf[pl.ds(ks,KB),:]=dk.astype(bf); dvf[pl.ds(ks,KB),:]=dv.astype(bf)
        return 0
    lax.fori_loop(0,nb-1,lambda j,_:block(j,False),0)
    block(nb-1,True)
    for i in range(0,nq,512):
        dq_ref[i:i+512,:]=(jnp.transpose(dqT[:,i:i+512])*0.125).astype(bf)
    for b in range(nq//piece):
        r=slice(b*piece,(b+1)*piece)
        y=x if b==0 else 1-x
        so=pl.ds((2*y+c)*piece,piece); ss=pl.ds((2*y+1-c)*piece,piece)
        dko_ref[r,:]=dkf[so,:]; dks_ref[r,:]=dkf[ss,:]
        dvo_ref[r,:]=dvf[so,:]; dvs_ref[r,:]=dvf[ss,:]

def attn_bwd(q, kvo, kvs, ctx, dctx, lse, sc, piece, KB=256, QB=512):
    nq,w=q.shape; pairs=w//128; L=2*kvo.shape[0]
    qspec=lambda off: pl.BlockSpec((nq,128),lambda p,s:(0,p+off))
    o=jax.ShapeDtypeStruct((nq,w),bf)
    V=pltpu.VMEM
    return pl.pallas_call(functools.partial(bwd_kernel,piece,KB,QB),
        grid_spec=pltpu.PrefetchScalarGridSpec(num_scalar_prefetch=1,grid=(pairs,),
            in_specs=[qspec(0),qspec(0),qspec(pairs),qspec(0),qspec(pairs),qspec(0),qspec(0),pl.BlockSpec((1,2,nq),lambda p,s:(p,0,0))],
            out_specs=[qspec(0)]*5,
            scratch_shapes=[V((L,128),bf)]*2+[V((128,L),bf)]*2+[V((128,nq),bf)]*4+[V((nq,128),bf)]*4+[V((2,nq),f32),V((L,128),bf),V((L,128),bf),V((128,nq),f32)]),
        out_shape=(o,)*5,
        name="attn_bwd",
        cost_estimate=pl.CostEstimate(flops=int(10*nq*L*w*0.6*3),bytes_accessed=12*nq*w*2*2,transcendentals=int(nq*L*w/64*0.6)),
        compiler_params=pltpu.CompilerParams(vmem_limit_bytes=48*2**20,dimension_semantics=("arbitrary",)))(sc,q,kvo,kvo,kvs,kvs,ctx,dctx,lse)

from jax.sharding import PartitionSpec as P
ALL=("dp","mp")
epsilon=1e-5
root_half=0.7071067811865476
inverse_root_two_pi=0.3989422804014327

def norm_forward(values, gain, shift):
    center = jnp.mean(values, axis=-1, keepdims=True)
    offset = values - center
    inverse = lax.rsqrt(jnp.mean(offset * offset, axis=-1, keepdims=True) + epsilon)
    normed = offset * inverse
    return (normed * gain + shift, normed, inverse)

def norm_backward(gradient, normed, inverse, gain):
    scaled = gradient * gain
    centered = (scaled - jnp.mean(scaled, axis=-1, keepdims=True)
        - normed * jnp.mean(scaled * normed, axis=-1, keepdims=True))
    return (inverse * centered, jnp.sum(gradient * normed, axis=0), jnp.sum(gradient, axis=0))

def dotT(a,b): return lax.dot_general(a,b,(((1,),(1,)),((),())),preferred_element_type=f32)
def Tdot(a,b): return lax.dot_general(a,b,(((0,),(0,)),((),())),preferred_element_type=f32)

XP=[(0,2),(2,0),(1,3),(3,1)]
CP=[(0,1),(1,0),(2,3),(3,2)]

def on_device(tokens, lengths, order, q_weight, k_weight, v_weight, o_weight, q_bias, v_bias, o_bias,
    attn_gain, attn_shift, in_weight, in_bias, out_weight, out_bias, ffn_gain, ffn_shift, cotangent):
    micro, rows, D = tokens.shape
    FF = in_weight.shape[1]
    G = lax.axis_size("dp")
    n = G*lax.axis_size("mp")
    g = lax.axis_index("dp"); m = lax.axis_index("mp")
    x = m//2; c = m%2
    sh = q_weight.shape[0]
    hw = D//2
    col = lambda v: v.reshape(sh,1)
    small = jnp.concatenate([col(v) for v in (q_bias,v_bias,o_bias,attn_gain,attn_shift,out_bias,ffn_gain,ffn_shift)]
        + [jnp.transpose(in_bias.reshape(FF//D,sh)), jnp.zeros((sh,128-8-FF//D),bf)],axis=1)
    qkv_l = jnp.concatenate([q_weight,k_weight,v_weight,small],axis=1)
    qkv = lax.all_gather(qkv_l,ALL,axis=0,tiled=True)
    oin = lax.all_gather(jnp.concatenate([o_weight,in_weight],axis=1),ALL,axis=0,tiled=True)
    w_out = lax.all_gather(out_weight,ALL,axis=0,tiled=True)
    w_o, w_in = oin[:,:D], oin[:,D:]
    smalls = jnp.transpose(qkv[:,3*D:])
    qb,vb,ob,ag,ash,outb,fg,fs = [smalls[i].astype(f32) for i in range(8)]
    inb = smalls[8:8+FF//D].reshape(FF//D,n,sh).transpose(1,0,2).reshape(FF).astype(f32)
    cut = lambda i: lax.dynamic_slice(qkv,(0,i*D+x*hw),(D,hw))
    wq,wk,wv = cut(0),cut(1),cut(2)
    qbx = lax.dynamic_slice(qb,(x*hw,),(hw,)); vbx = lax.dynamic_slice(vb,(x*hw,),(hw,))
    R = rows//G
    mixed = lax.all_to_all(tokens.reshape(micro,G,R,D),"dp",split_axis=1,concat_axis=0,tiled=True).reshape(micro*G,R,D)
    picked = jnp.take(mixed,order,axis=0).reshape(G,micro,R,D)
    live_all = jnp.take(lengths,order,axis=0)
    outs=[];igs=[]
    st=[]
    for s in range(micro):
        own = lax.all_to_all(picked[:,s],"dp",split_axis=0,concat_axis=0,tiled=True).reshape(rows,D)
        oth = lax.ppermute(own,"mp",XP)
        X = jnp.concatenate([own,oth],axis=0)
        live = live_all[g*micro+s]
        sc = jnp.stack([live,c,x]).astype(jnp.int32)
        q = (jnp.dot(X,wq,preferred_element_type=f32)+qbx).astype(bf)
        k = jnp.dot(X,wk,preferred_element_type=f32).astype(bf)
        v = (jnp.dot(X,wv,preferred_element_type=f32)+vbx).astype(bf)
        kvo = jnp.concatenate([k,v],axis=1)
        kvs = lax.ppermute(kvo,"mp",CP)
        ctx,lse = attn_fwd(q,kvo,kvs,sc,rows)
        c_oth = lax.ppermute(ctx[rows:],"mp",XP)
        st.append([own,X,sc,q,kvo,kvs,ctx,lse,c_oth])
    dW=None
    st2=[]
    for s in range(micro):
        own,X,sc,q,kvo,kvs,ctx,lse,c_oth = st[s]
        mine = ctx[:rows]
        cfull = jnp.where(x==0,jnp.concatenate([mine,c_oth],axis=1),jnp.concatenate([c_oth,mine],axis=1))
        A = own.astype(f32)+jnp.dot(cfull,w_o,preferred_element_type=f32)+ob
        U,n1,r1 = norm_forward(A,ag,ash)
        ul = U.astype(bf)
        F = jnp.dot(ul,w_in,preferred_element_type=f32)+inb
        Z = jax.nn.gelu(F,approximate=False).astype(bf)
        B = U+jnp.dot(Z,w_out,preferred_element_type=f32)+outb
        out,n2,r2 = norm_forward(B,fg,fs)
        outs.append(out.astype(bf))
        G_ = cotangent[s].astype(f32)
        dB,dfg,dfs = norm_backward(G_,n2,r2,fg)
        dO = dB.astype(bf)
        doutb = jnp.sum(dO.astype(f32),axis=0)
        dwout = Tdot(Z,dO)
        dZ = dotT(dO,w_out)
        slope = 0.5*(1.0+lax.erf(F*root_half))+F*jnp.exp(-0.5*F*F)*inverse_root_two_pi
        dF = (dZ*slope).astype(bf)
        dinb = jnp.sum(dF.astype(f32),axis=0)
        dwin = Tdot(ul,dF)
        dU = dB+dotT(dF,w_in)
        dA,dag,dash = norm_backward(dU,n1,r1,ag)
        dM = dA.astype(bf)
        dob = jnp.sum(dM.astype(f32),axis=0)
        dwo = Tdot(cfull,dM)
        dC = dotT(dM,w_o).astype(bf)
        dc_l,dc_r = dC[:,:hw],dC[:,hw:]
        keep = jnp.where(x==0,dc_l,dc_r); send = jnp.where(x==0,dc_r,dc_l)
        got = lax.ppermute(send,"mp",XP)
        st2.append((dA,jnp.concatenate([keep,got],axis=0)))
        now = [dwo,dwin,dwout,dob,dag,dash,doutb,dfg,dfs,dinb]
        dW = now if dW is None else [a+b for a,b in zip(dW,now)]
    dQKV=None
    for s in range(micro):
        own,X,sc,q,kvo,kvs,ctx,lse,c_oth = st[s]
        dA,dctx = st2[s]
        dq,dko,dvo,dks,dvs = attn_bwd(q,kvo,kvs,ctx,dctx,lse,sc,rows)
        r_ = lax.ppermute(jnp.concatenate([dks,dvs],axis=1),"mp",CP)
        dk = (dko.astype(f32)+r_[:,:hw].astype(f32)).astype(bf)
        dv = (dvo.astype(f32)+r_[:,hw:].astype(f32)).astype(bf)
        dXp = dotT(dq,wq)+dotT(dk,wk)+dotT(dv,wv)
        rx = lax.ppermute(dXp[rows:].astype(bf),"mp",XP)
        igs.append(dA+dXp[:rows]+rx.astype(f32))
        now = [Tdot(X,dq),Tdot(X,dk),Tdot(X,dv),jnp.sum(dq.astype(f32),axis=0),jnp.sum(dv.astype(f32),axis=0)]
        dQKV = now if dQKV is None else [a+b for a,b in zip(dQKV,now)]
    wide = lambda t: lax.dynamic_update_slice(jnp.zeros(t.shape[:-1]+(D,),bf),t.astype(bf),(0,)*(t.ndim-1)+(x*hw,))
    dwq,dwk,dwv,dqb,dvb = [wide(t) for t in dQKV]
    dwo,dwin,dwout,dob,dag,dash,doutb,dfg,dfs,dinb = [t.astype(bf) for t in dW]
    dsm = jnp.concatenate([jnp.stack([dqb,dvb,dob,dag,dash,doutb,dfg,dfs]),
        dinb.reshape(n,FF//D,sh).transpose(1,0,2).reshape(FF//D,D), jnp.zeros((128-8-FF//D,D),bf)],axis=0)
    dwo2 = dwout.reshape(n,FF//D,sh,D).transpose(0,2,1,3).reshape(D,FF)
    big = jnp.concatenate([dwq,dwk,dwv,dwo,dwin,dwo2,jnp.transpose(dsm)],axis=1)
    red = lax.psum_scatter(big,ALL,scatter_dimension=0,tiled=True).astype(f32)
    pick = lambda i: red[:,i*D:(i+1)*D]
    gin = red[:,4*D:4*D+FF]
    gout = red[:,4*D+FF:4*D+2*FF].reshape(sh,FF//D,D).transpose(1,0,2).reshape(sh*(FF//D),D)
    sm = jnp.transpose(red[:,4*D+2*FF:])
    ginb = sm[8:8+FF//D].reshape(-1)
    return (jnp.stack(outs),jnp.stack(igs),pick(0),pick(1),pick(2),pick(3),sm[0],sm[1],sm[2],sm[3],sm[4],gin,ginb,gout,sm[5],sm[6],sm[7])

def solution(mesh):
    r2=P(ALL,None); r1=P(ALL); t=P("dp","mp",None)
    return jax.shard_map(on_device,mesh=mesh,
        in_specs=(t,P(),P(),r2,r2,r2,r2,r1,r1,r1,r1,r1,r2,r1,r2,r1,r1,r1,t),
        out_specs=(t,t,r2,r2,r2,r2,r1,r1,r1,r1,r1,r2,r1,r2,r1,r1,r1),check_vma=False)
```

time: 1750 us -> 651 us (0.37)
  waiting for transfers between devices: 845 us -> 240 us
  matrix products: 530 us -> 148 us
  Pallas kernels: 0 us -> 89.7 us
  local copies, waits for them, and re-layouts: 150 us -> 68.3 us
  blocking collectives: 98.6 us -> 33.2 us
  other arithmetic: 84.4 us -> 28.3 us
    reduce_scatter x10 -> x0, waiting for transfers between devices: 702 us -> none  [the longest x1 142 us: on_device(): lax.psum_scatter(running[9], ('dp', 'mp'), scatter_dimension=0, tiled=True)]
    dot_general x204 -> x36, matrix products: 530 us -> 148 us  [the longest x12 45.1 us: Tdot(): lax.dot_general(a, b, (((0,), (0,)), ((), ())), preferred_element_type=f32)]
    unnamed x20 -> x5, waiting for transfers between devices: 5.21 us -> 123 us
    all_gather x10 -> x3, waiting for transfers between devices: 101 us -> 0.02 us  [the longest x1 0.02 us: on_device(): w_out = lax.all_gather(out_weight, ALL, axis=0, tiled=True)]
    unnamed x2 -> x0, blocking collectives: 98.6 us -> none
    pallas_call x0 -> x4, Pallas kernels: none -> 89.7 us  [the longest x2 53.2 us: attn_bwd(): pl.pallas_call(functools.partial(bwd_kernel, piece, KB, QB), grid_spec=pl...]
    ppermute x0 -> x12, waiting for transfers between devices: none -> 51.8 us  [the longest x2 27.8 us: on_device(): rx = lax.ppermute(dXp[rows:].astype(bf), 'mp', XP)]
    while x48 -> x0, local copies, waits for them, and re-layouts: 47 us -> none
  transfers between devices with their start and end apart: 22 -> 18, of which waited for: 14 -> 7; matrix products, arithmetic and copies ran while one was open for 30% -> 20% of each run, Pallas kernels for 0% -> 14%
where the time goes in v1:
time: 651 us; the launch traced here: 644 us
  waiting for transfers between devices  240 us (37%)
  matrix products  148 us (23%)
  Pallas kernels  89.7 us (14%)
  local copies, waits for them, and re-layouts  68.3 us (10%)
  blocking collectives  33.2 us (5%)
  other arithmetic  28.3 us (4%)
  starting transfers between devices  21.3 us (3%)
  between operations  15.2 us (2%)
    unnamed x5, waiting for transfers between devices  123 us
    pallas_call x2, Pallas kernels, attn_bwd(): pl.pallas_call(functools.partial(bwd_kernel, piece, KB, QB), grid_spec=pl...  53.2 us
    dot_general x12, matrix products, Tdot(): lax.dot_general(a, b, (((0,), (0,)), ((), ())), preferred_element_type=f32)  45.1 us
    all_to_all x1, waiting for transfers between devices, on_device(): lax.all_to_all(tokens.reshape(micro, G, R, D), 'dp', split_axis=1, concat...  43.7 us
    dot_general x12, matrix products, dotT(): lax.dot_general(a, b, (((1,), (1,)), ((), ())), preferred_element_type=f32)  40.8 us
    pallas_call x2, Pallas kernels, attn_fwd(): pl.pallas_call(functools.partial(fwd_kernel, piece, KB, QB), grid_spec=pl...  36.5 us
    dot_general x2, matrix products, on_device(): F = jnp.dot(ul, w_in, preferred_element_type=f32) + inb  34.5 us
    all_to_all x1, blocking collectives, on_device(): lax.all_to_all(picked[:, s], 'dp', split_axis=0, concat_axis=0, tiled=True)  33.2 us
  transfers between devices with their start and end apart: 18, of which 7 were waited for; matrix products, arithmetic and copies ran while one was open for 20% of the time, Pallas kernels for 14%

profile of v1, /device:TPU:0, one launch (start us, length us, event | category | flops | bytes accessed | tf_op | source)
XLA Modules:
  0.0 643.9 jit_solution(16738420600433781466)
XLA Ops:
  17.3 2.7 copy.118
  20.0 7.4 %all-to-all-start = ((bf16[2,8,64,768]{3,2,0,1:T(8,128)(2,1)}), bf16[2,8,64,768]{3,2,0,1:T(8,128)(2,1)S(1)}, u32[]{:S(2)}, u32[]{:S(2)}) async-start(bf16[2,8,64,768]{3,2,0,1:T(8,128)(2,1)} %copy.118), calls=%async_computation | async-start | bytes 3145728 | tf_op jit(solution)/shard_map/all_to_all | solution.py:207
  28.2 43.7 %all-to-all-done = bf16[2,8,64,768]{3,2,0,1:T(8,128)(2,1)S(1)} async-done(((bf16[2,8,64,768]{3,2,0,1:T(8,128)(2,1)}), bf16[2,8,64,768]{3,2,0,1:T(8,128)(2,1)S(1)}, u32[]{:S(2)}, u32[]{:S(2)}) %all-to-all-start) | async-done | bytes 1572896 | tf_op jit(solution)/shard_map/all_to_all | solution.py:207
  73.8 33.2 %all_to_all.25 = bf16[8,64,768]{2,1,0:T(8,128)(2,1)S(1)} all-to-all(bf16[8,64,768]{2,1,0:T(8,128)(2,1)S(1)} %get-tuple-element.92), channel_id=1, replica_groups=mesh['dp'=8,'mp'=4] {'dp'}, dimensions={0} | all-to-all | bytes 1572864 | tf_op jit(solution)/shard_map/all_to_all | solution.py:213
  107.0 3.6 all-to-all-start.2
  113.1 21.7 %all-to-all-done.2 = bf16[8,64,768]{2,1,0:T(8,128)(2,1)S(1)} async-done(((bf16[8,64,768]{2,1,0:T(8,128)(2,1)}), bf16[8,64,768]{2,1,0:T(8,128)(2,1)S(1)}, u32[]{:S(2)}, u32[]{:S(2)}) %all-to-all-start.2) | async-done | bytes 786464 | tf_op jit(solution)/shard_map/all_to_all | solution.py:213
  138.1 2.3 convolution_convert_fusion.3
  140.4 2.3 add_convert_fusion.11
  142.9 15.3 %collective-permute-done.3 = bf16[512,768]{1,0:T(8,128)(2,1)} collective-permute-done((bf16[512,768]{1,0:T(8,128)(2,1)S(1)}, bf16[512,768]{1,0:T(8,128)(2,1)}, u32[]{:S(2)}, u32[]{:S(2)}) %collective-permute-start.3) | collective-permute-done | bytes 786464 | tf_op jit(solution)/shard_map/ppermute | solution.py:214
  158.2 2.3 convolution_convert_fusion.2
  160.5 2.4 add_convert_fusion.8
  169.3 2.6 add_convert_fusion.9.q_ref
  171.9 2.6 add_convert_fusion.12.q_ref
  174.6 27.1 %attn_fwd.2 = (bf16[1024,384]{1,0:T(8,128)(2,1)S(1)}, f32[3,2,1024]{2,1,0:T(2,128)S(1)}) custom-call(s32[3]{0:T(128)S(1)} %add_add_fusion.6.live_ref, bf16[1024,384]{1,0:T(8,128)(2,1)S(1)} %add_convert_fusion.12.q_ref, bf16[1024,768]{1,0:T(8,128)(2,1)S(1)} %pad_maximum_fusion.2.ko_ref.vo_ref, bf16[1024,768]{1,0:T(8,128)(2,1)S(1)} %pad_maximum_fusion.2.ko_ref.vo_ref, ...), custom_call_target="tpu_custom_call" | custom-call | flops 5798205952 | bytes 9437184 | tf_op jit(solution)/shard_map/attn_fwd/pallas_call | solution.py:71
  204.0 9.4 %attn_fwd.3 = (bf16[1024,384]{1,0:T(8,128)(2,1)S(1)}, f32[3,2,1024]{2,1,0:T(2,128)S(1)}) custom-call(s32[3]{0:T(128)S(1)} %add_add_fusion.7.live_ref, bf16[1024,384]{1,0:T(8,128)(2,1)S(1)} %add_convert_fusion.9.q_ref, bf16[1024,768]{1,0:T(8,128)(2,1)S(1)} %pad_maximum_fusion.4.ko_ref.vo_ref, bf16[1024,768]{1,0:T(8,128)(2,1)S(1)} %pad_maximum_fusion.4.ko_ref.vo_ref, ...), custom_call_target="tpu_custom_call" | custom-call | flops 5798205952 | bytes 9437184 | tf_op jit(solution)/shard_map/attn_fwd/pallas_call | solution.py:71
  215.1 2.6 fusion.144
  218.1 8.6 %collective-permute-done.5 = bf16[512,384]{1,0:T(8,128)(2,1)S(1)} collective-permute-done((bf16[512,384]{1,0:T(8,128)(2,1)S(1)}, bf16[512,384]{1,0:T(8,128)(2,1)S(1)}, u32[]{:S(2)}, u32[]{:S(2)}) %collective-permute-start.5) | collective-permute-done | bytes 393248 | tf_op jit(solution)/shard_map/ppermute | solution.py:224
  228.0 2.7 fusion.37
  230.7 2.7 copy-done.65
  233.5 31.8 %fusion.2 = (bf16[512,3072]{1,0:T(8,128)(2,1)}, bf16[512,3072]{1,0:T(8,128)(2,1)S(1)}, f32[512,3072]{1,0:T(8,128)}) fusion(f32[3072]{0:T(1024)S(1)} %reshape.359, f32[512,3072]{1,0:T(8,128)S(1)} %fusion.37, bf16[768,3840]{1,0:T(8,128)(2,1)S(1)} %copy-done.61, f32[512,768]{1,0:T(8,128)S(1)} %get-tuple-element.119, f32[768]{0:T(1024)S(1)} %get-tuple-element.66, ...), kind=kOutput, calls=%fused_computation.10 | convolution fusion | flops 2625503232 | bytes 25190400 | tf_op jit(solution)/shard_map/dot_general | solution.py:235
  265.3 6.6 %fusion.146 = (f32[512]{0:T(512)S(1)}, f32[512,768]{1,0:T(8,128)S(1)}) fusion(f32[768]{0:T(1024)S(1)} %get-tuple-element.65, bf16[512,3072]{1,0:T(8,128)(2,1)} %get-tuple-element.110, bf16[3072,768]{1,0:T(8,128)(2,1)} %all-gather.8.cloned.1.call-done, f32[768]{0:T(1024)S(1)} %get-tuple-element.66, f32[768]{0:T(1024)S(1)} %get-tuple-element.67, ...), kind=kOutput, calls=%fused_computation.296 | convolution fusion | flops 2418671104 | bytes 11025408 | tf_op jit(solution)/shard_map/dot_general | solution.py:237
  273.3 2.8 fusion.147
  280.0 2.3 convert_reduce_fusion.4
  282.4 6.1 fusion.126
  288.5 5.6 convert_reduce_fusion.1
  294.2 5.8 convert_reduce_fusion
  301.9 7.4 %multiply_reduce_fusion.1 = (f32[768]{0:T(1024)S(1)}, f32[512]{0:T(512)S(1)}, f32[512]{0:T(512)S(1)}, f32[768]{0:T(1024)S(1)}, f32[512,768]{1,0:T(8,128)S(1)}) fusion(f32[512,768]{1,0:T(8,128)} %copy-done.40, f32[512]{0:T(512)S(1)} %add_rsqrt_fusion.3, f32[512]{0:T(512)S(1)} %broadcast_multiply_fusion.11, f32[768]{0:T(1024)S(1)} %get-tuple-element.67, ...), kind=kOutput, calls=%fused_computation.111 | convolution fusion | flops 2419848704 | bytes 12600320 | tf_op jit(solution)/shard_map/dot_general | solution.py:176
  309.3 5.9 convert_reduce_fusion.7
  327.6 3.1 add_convert_fusion.2
  330.7 2.3 copy.146
  333.0 6.0 add_convert_fusion
  339.0 2.3 copy.136
  341.4 3.3 copy.153
  344.7 5.6 fusion.132
  352.4 14.0 %attn_bwd.3 = (bf16[1024,384]{1,0:T(8,128)(2,1)S(1)}, bf16[1024,384]{1,0:T(8,128)(2,1)S(1)}, bf16[1024,384]{1,0:T(8,128)(2,1)S(1)}, bf16[1024,384]{1,0:T(8,128)(2,1)S(1)}, bf16[1024,384]{1,0:T(8,128)(2,1)S(1)}) custom-call(s32[3]{0:T(128)S(1)} %add_add_fusion.7.live_ref, bf16[1024,384]{1,0:T(8,128)(2,1)S(1)} %copy-done.17, bf16[1024,768]{1,0:T(8,128)(2,1)} %copy-done.3, ...), custom_call_target="tpu_custom_call" | custom-call | flops 14495514624 | bytes 18874368 | tf_op jit(solution)/shard_map/attn_bwd/pallas_call | solution.py:147
  369.9 39.2 %attn_bwd.2 = (bf16[1024,384]{1,0:T(8,128)(2,1)S(1)}, bf16[1024,384]{1,0:T(8,128)(2,1)S(1)}, bf16[1024,384]{1,0:T(8,128)(2,1)S(1)}, bf16[1024,384]{1,0:T(8,128)(2,1)S(1)}, bf16[1024,384]{1,0:T(8,128)(2,1)S(1)}) custom-call(s32[3]{0:T(128)S(1)} %add_add_fusion.6.live_ref, bf16[1024,384]{1,0:T(8,128)(2,1)S(1)} %copy-done.15, bf16[1024,768]{1,0:T(8,128)(2,1)} %copy-done.2, ...), custom_call_target="tpu_custom_call" | custom-call | flops 14495514624 | bytes 18874368 | tf_op jit(solution)/shard_map/attn_bwd/pallas_call | solution.py:147
  413.0 2.9 fusion.71
  421.7 2.3 fusion.102
  424.1 3.1 fusion.72
  429.2 2.5 fusion.129
  431.8 3.1 fusion.73
  446.6 7.5 %fusion.32 = bf16[768,9344]{1,0:T(8,128)(2,1)} fusion(bf16[768,9344]{1,0:T(8,128)(2,1)} %constant_dynamic-update-slice_fusion.1, f32[768,3072]{1,0:T(8,128)} %fusion.132, bf16[512,3072]{1,0:T(8,128)(2,1)S(1)} %copy-done.67, f32[512,768]{1,0:T(8,128)S(1)} %copy-done.26, f32[512]{0:T(512)S(1)} %add_rsqrt_fusion.1, f32[512]{0:T(512)S(1)} %broadcast_multiply_fusion.9, ...), kind=kOutput, calls=%fused_computation.58 | convolution fusion | flops 2422603776 | bytes 18884608 | tf_op jit(solution)/shard_map/dot_general | solution.py:177
  454.2 2.5 constant_dynamic-update-slice_fusion
  457.4 3.3 concatenate.62
  468.0 2.2 add_add_fusion.1
  478.8 12.0 %collective-permute-done.8 = bf16[512,768]{1,0:T(8,128)(2,1)S(1)} collective-permute-done((bf16[512,768]{1,0:T(8,128)(2,1)S(1)}, bf16[512,768]{1,0:T(8,128)(2,1)S(1)}, u32[]{:S(2)}, u32[]{:S(2)}) %collective-permute-start.8) | collective-permute-done | bytes 786464 | tf_op jit(solution)/shard_map/ppermute | solution.py:271
  491.0 15.9 %collective-permute-done.11 = bf16[512,768]{1,0:T(8,128)(2,1)S(1)} collective-permute-done((bf16[512,768]{1,0:T(8,128)(2,1)S(1)}, bf16[512,768]{1,0:T(8,128)(2,1)S(1)}, u32[]{:S(2)}, u32[]{:S(2)}) %collective-permute-start.11) | collective-permute-done | bytes 786464 | tf_op jit(solution)/shard_map/ppermute | solution.py:271
  509.0 123.0 %reduce-scatter.4.cloned.1.call-done = bf16[24,9344]{1,0:T(8,128)(2,1)} async-done(((bf16[768,9344]{1,0:T(8,128)(2,1)}), bf16[24,9344]{1,0:T(8,128)(2,1)}) %reduce-scatter.4.cloned.1.call-update) | async-done | bytes 448528
  (315 shorter events, 103.0 us)
Async XLA Ops:
  7.2 20.3 %copy-start = (s32[16]{0:T(128)S(1)}, s32[16]{0:T(128)}, u32[]{:S(2)}) copy-start(s32[16]{0:T(128)} %param.20) | copy-start | bytes 196
  7.2 129.1 %all-gather.4.cloned.1.call-start = ((), (), s32[]{:S(2)}) async-start(), calls=%async_computation.4 | async-start | bytes 3852288 | tf_op jit(solution)/shard_map/all_gather | solution.py:196
  15.7 199.5 %all-gather.6.cloned.1.call-start = ((), (), s32[]{:S(2)}) async-start(), calls=%async_computation.5 | async-start | bytes 6082560 | tf_op jit(solution)/shard_map/all_gather | solution.py:197
  20.0 7.4 %copy-start.60 = (s32[16]{0:T(128)S(1)}, s32[16]{0:T(128)}, u32[]{:S(2)}) copy-start(s32[16]{0:T(128)} %param.21) | copy-start | bytes 196
  20.0 51.9 %all-to-all-start = ((bf16[2,8,64,768]{3,2,0,1:T(8,128)(2,1)}), bf16[2,8,64,768]{3,2,0,1:T(8,128)(2,1)S(1)}, u32[]{:S(2)}, u32[]{:S(2)}) async-start(bf16[2,8,64,768]{3,2,0,1:T(8,128)(2,1)} %copy.118), calls=%async_computation | async-start | bytes 3145728 | tf_op jit(solution)/shard_map/all_to_all | solution.py:207
  73.8 39.1 %copy-start.18 = (bf16[2,512,768]{2,1,0:T(8,128)(2,1)S(1)}, bf16[2,512,768]{2,1,0:T(8,128)(2,1)}, u32[]{:S(2)}) copy-start(bf16[2,512,768]{2,1,0:T(8,128)(2,1)} %param.37) | copy-start | bytes 4718596
  107.0 33.4 %copy-start.48 = (bf16[8,64,768]{2,1,0:T(8,128)(2,1)}, bf16[8,64,768]{2,1,0:T(8,128)(2,1)S(1)}, u32[]{:S(2)}) copy-start(bf16[8,64,768]{2,1,0:T(8,128)(2,1)S(1)} %all_to_all.25) | copy-start | bytes 2359300
  107.0 27.8 %all-to-all-start.2 = ((bf16[8,64,768]{2,1,0:T(8,128)(2,1)}), bf16[8,64,768]{2,1,0:T(8,128)(2,1)S(1)}, u32[]{:S(2)}, u32[]{:S(2)}) async-start(bf16[8,64,768]{2,1,0:T(8,128)(2,1)} %get-tuple-element.93), calls=%async_computation.2 | async-start | bytes 1572864 | tf_op jit(solution)/shard_map/all_to_all | solution.py:213
  110.6 154.6 %all-gather.8.cloned.1.call-start = ((), (), s32[]{:S(2)}) async-start(), calls=%async_computation.6 | async-start | bytes 4866048 | tf_op jit(solution)/shard_map/all_gather | solution.py:198
  110.6 27.5 %collective-permute-start = (bf16[512,768]{1,0:T(8,128)(2,1)S(1)}, bf16[512,768]{1,0:T(8,128)(2,1)}, u32[]{:S(2)}, u32[]{:S(2)}) collective-permute-start(bf16[512,768]{1,0:T(8,128)(2,1)S(1)} %bitcast.118), channel_id=1, source_target_pairs={{0,2},{2,0},{1,3},{3,1},{4,6},{6,4},{5,7},{7,5},{8,10},{10,8},{9,1... | collective-permute-start | bytes 2359304 | tf_op jit(solution)/shard_map/ppermute | solution.py:214
  112.2 519.8 %reduce-scatter.4.cloned.1.call-start = ((), (), s32[]{:S(2)}) async-start(), calls=%async_computation.7 | async-start | bytes 14800896
  134.9 25.7 %copy-start.54 = (bf16[8,64,768]{2,1,0:T(8,128)(2,1)}, bf16[8,64,768]{2,1,0:T(8,128)(2,1)S(1)}, u32[]{:S(2)}) copy-start(bf16[8,64,768]{2,1,0:T(8,128)(2,1)S(1)} %all-to-all-done.2) | copy-start | bytes 2359300
  134.9 23.4 %collective-permute-start.3 = (bf16[512,768]{1,0:T(8,128)(2,1)S(1)}, bf16[512,768]{1,0:T(8,128)(2,1)}, u32[]{:S(2)}, u32[]{:S(2)}) collective-permute-start(bf16[512,768]{1,0:T(8,128)(2,1)S(1)} %bitcast.126), channel_id=1, source_target_pairs={{0,2},{2,0},{1,3},{3,1},{4,6},{6,4},{5,7},{7,5},{8,10},{10,8},{9,1... | collective-permute-start | bytes 2359304 | tf_op jit(solution)/shard_map/ppermute | solution.py:214
  142.8 31.7 %copy-start.2 = (bf16[1024,768]{1,0:T(8,128)(2,1)}, bf16[1024,768]{1,0:T(8,128)(2,1)S(1)}, u32[]{:S(2)}) copy-start(bf16[1024,768]{1,0:T(8,128)(2,1)S(1)} %pad_maximum_fusion.2.ko_ref.vo_ref) | copy-start | bytes 4718596
  142.9 31.7 %collective-permute-start.1 = (bf16[1024,768]{1,0:T(8,128)(2,1)S(1)}, bf16[1024,768]{1,0:T(8,128)(2,1)}, u32[]{:S(2)}, u32[]{:S(2)}) collective-permute-start(bf16[1024,768]{1,0:T(8,128)(2,1)S(1)} %pad_maximum_fusion.2.ko_ref.vo_ref), channel_id=1, source_target_pairs={{0,1},{1,0},{2,3},{3,2},{4,5},{5,4},{6,7},{7,6},{8,9},{9,8},{10,11... | collective-permute-start | bytes 4718600 | tf_op jit(solution)/shard_map/ppermute | solution.py:222
  163.1 40.9 %copy-start.3 = (bf16[1024,768]{1,0:T(8,128)(2,1)}, bf16[1024,768]{1,0:T(8,128)(2,1)S(1)}, u32[]{:S(2)}) copy-start(bf16[1024,768]{1,0:T(8,128)(2,1)S(1)} %pad_maximum_fusion.4.ko_ref.vo_ref) | copy-start | bytes 4718596
  163.1 40.9 %collective-permute-start.4 = (bf16[1024,768]{1,0:T(8,128)(2,1)S(1)}, bf16[1024,768]{1,0:T(8,128)(2,1)}, u32[]{:S(2)}, u32[]{:S(2)}) collective-permute-start(bf16[1024,768]{1,0:T(8,128)(2,1)S(1)} %pad_maximum_fusion.4.ko_ref.vo_ref), channel_id=1, source_target_pairs={{0,1},{1,0},{2,3},{3,2},{4,5},{5,4},{6,7},{7,6},{8,9},{9,8},{10,11... | collective-permute-start | bytes 4718600 | tf_op jit(solution)/shard_map/ppermute | solution.py:222
  171.9 32.1 %copy-start.16 = (bf16[1024,384]{1,0:T(8,128)(2,1)}, bf16[1024,384]{1,0:T(8,128)(2,1)S(1)}, u32[]{:S(2)}) copy-start(bf16[1024,384]{1,0:T(8,128)(2,1)S(1)} %add_convert_fusion.9.q_ref) | copy-start | bytes 2359300
  174.5 27.1 %copy-start.14 = (bf16[1024,384]{1,0:T(8,128)(2,1)}, bf16[1024,384]{1,0:T(8,128)(2,1)S(1)}, u32[]{:S(2)}) copy-start(bf16[1024,384]{1,0:T(8,128)(2,1)S(1)} %add_convert_fusion.12.q_ref) | copy-start | bytes 2359300
  202.7 12.4 %copy-start.43 = (bf16[512,384]{1,0:T(8,128)(2,1)}, bf16[512,384]{1,0:T(8,128)(2,1)S(1)}, u32[]{:S(2)}) copy-start(bf16[512,384]{1,0:T(8,128)(2,1)S(1)} %get-tuple-element.98) | copy-start | bytes 1179652
  202.7 12.4 %collective-permute-start.2 = (bf16[512,384]{1,0:T(8,128)(2,1)S(1)}, bf16[512,384]{1,0:T(8,128)(2,1)}, u32[]{:S(2)}, u32[]{:S(2)}) collective-permute-start(bf16[512,384]{1,0:T(8,128)(2,1)S(1)} %get-tuple-element.99), channel_id=1, source_target_pairs={{0,2},{2,0},{1,3},{3,1},{4,6},{6,4},{5,7},{7,5},{8,10},{10,8},{9,1... | collective-permute-start | bytes 1179656 | tf_op jit(solution)/shard_map/ppermute | solution.py:224
  214.4 12.3 %copy-start.58 = (bf16[512,384]{1,0:T(8,128)(2,1)}, bf16[512,384]{1,0:T(8,128)(2,1)S(1)}, u32[]{:S(2)}) copy-start(bf16[512,384]{1,0:T(8,128)(2,1)S(1)} %get-tuple-element.100) | copy-start | bytes 1179652
  214.4 12.3 %collective-permute-start.5 = (bf16[512,384]{1,0:T(8,128)(2,1)S(1)}, bf16[512,384]{1,0:T(8,128)(2,1)S(1)}, u32[]{:S(2)}, u32[]{:S(2)}) collective-permute-start(bf16[512,384]{1,0:T(8,128)(2,1)S(1)} %get-tuple-element.101), channel_id=1, source_target_pairs={{0,2},{2,0},{1,3},{3,1},{4,6},{6,4},{5,7},{7,5},{8,10},{10,8},{9,1... | collective-permute-start | bytes 1179656 | tf_op jit(solution)/shard_map/ppermute | solution.py:224
  215.1 11.6 %copy-start.61 = (bf16[768,3840]{1,0:T(8,128)(2,1)S(1)}, bf16[768,3840]{1,0:T(8,128)(2,1)}, u32[]{:S(2)}) copy-start(bf16[768,3840]{1,0:T(8,128)(2,1)} %all-gather.6.cloned.1.call-done) | copy-start | bytes 17694724
  217.7 13.0 %copy-start.40 = (f32[512,768]{1,0:T(8,128)}, f32[512,768]{1,0:T(8,128)S(1)}, u32[]{:S(2)}) copy-start(f32[512,768]{1,0:T(8,128)S(1)} %get-tuple-element.119) | copy-start | bytes 4718596
  217.7 9.0 %copy-start.55 = (bf16[8,64,768]{2,1,0:T(8,128)(2,1)S(1)}, bf16[8,64,768]{2,1,0:T(8,128)(2,1)}, u32[]{:S(2)}) copy-start(bf16[8,64,768]{2,1,0:T(8,128)(2,1)} %copy-done.54) | copy-start | bytes 2359300
  265.3 7.0 %slice-start.2 = ((s8[4718592]{0:T(1024)(128)(4,1)}), s8[4194304]{0:T(1024)(128)(4,1)S(1)}, s32[]{:S(2)}) async-start(s8[4718592]{0:T(1024)(128)(4,1)} %bitcast.147), calls=%async_computation.10 | async-start | bytes 8388608
  265.3 7.0 %slice-start.3 = ((s8[4718592]{0:T(1024)(128)(4,1)}), s8[524288]{0:T(1024)(128)(4,1)S(1)}, s32[]{:S(2)}) async-start(s8[4718592]{0:T(1024)(128)(4,1)} %bitcast.147), calls=%async_computation.11 | async-start | bytes 1048576
  280.0 8.5 %slice-start.6 = ((s8[6291456]{0:T(1024)(128)(4,1)}), s8[4194304]{0:T(1024)(128)(4,1)S(1)}, s32[]{:S(2)}) async-start(s8[6291456]{0:T(1024)(128)(4,1)} %bitcast.151), calls=%async_computation.14 | async-start | bytes 8388608
  282.3 6.2 copy-start.22
  282.4 11.8 %copy-start.20 = (f32[512,768]{1,0:T(8,128)}, f32[512,768]{1,0:T(8,128)S(1)}, u32[]{:S(2)}) copy-start(f32[512,768]{1,0:T(8,128)S(1)} %get-tuple-element.78) | copy-start | bytes 4718596
  282.4 11.8 %slice-start.4 = ((s8[6291456]{0:T(1024)(128)(4,1)}), s8[4194304]{0:T(1024)(128)(4,1)S(1)}, s32[]{:S(2)}) async-start(s8[6291456]{0:T(1024)(128)(4,1)} %bitcast.149), calls=%async_computation.12 | async-start | bytes 8388608
  301.9 7.4 %copy-start.21 = (f32[512,768]{1,0:T(8,128)S(1)}, f32[512,768]{1,0:T(8,128)}, u32[]{:S(2)}) copy-start(f32[512,768]{1,0:T(8,128)} %copy-done.20) | copy-start | bytes 4718596
  301.9 7.4 %copy-start.25 = (f32[512,768]{1,0:T(8,128)S(1)}, f32[512,768]{1,0:T(8,128)}, u32[]{:S(2)}) copy-start(f32[512,768]{1,0:T(8,128)} %copy-done.23) | copy-start | bytes 4718596
  301.9 7.4 %copy-start.41 = (f32[512,768]{1,0:T(8,128)S(1)}, f32[512,768]{1,0:T(8,128)}, u32[]{:S(2)}) copy-start(f32[512,768]{1,0:T(8,128)} %copy-done.40) | copy-start | bytes 4718596
  301.9 7.4 %copy-start.66 = (bf16[512,3072]{1,0:T(8,128)(2,1)S(1)}, bf16[512,3072]{1,0:T(8,128)(2,1)}, u32[]{:S(2)}) copy-start(bf16[512,3072]{1,0:T(8,128)(2,1)} %get-tuple-element.132) | copy-start | bytes 9437188
  315.2 12.4 %copy-start.27 = (f32[512,768]{1,0:T(8,128)}, f32[512,768]{1,0:T(8,128)S(1)}, u32[]{:S(2)}) copy-start(f32[512,768]{1,0:T(8,128)S(1)} %get-tuple-element.84) | copy-start | bytes 4718596
  315.8 11.0 %copy-start.29 = (f32[512,768]{1,0:T(8,128)}, f32[512,768]{1,0:T(8,128)S(1)}, u32[]{:S(2)}) copy-start(f32[512,768]{1,0:T(8,128)S(1)} %get-tuple-element.82) | copy-start | bytes 4718596
  324.7 25.6 %collective-permute-start.9 = (bf16[512,384]{1,0:T(8,128)(2,1)}, bf16[512,384]{1,0:T(8,128)(2,1)}, u32[]{:S(2)}, u32[]{:S(2)}) collective-permute-start(bf16[512,384]{1,0:T(8,128)(2,1)} %get-tuple-element.97), channel_id=1, source_target_pairs={{0,2},{2,0},{1,3},{3,1},{4,6},{6,4},{5,7},{7,5},{8,10},{10,8},{9,1... | collective-permute-start | bytes 1179656 | tf_op jit(solution)/shard_map/ppermute | solution.py:258
  326.1 41.7 %collective-permute-start.6 = (bf16[512,384]{1,0:T(8,128)(2,1)}, bf16[512,384]{1,0:T(8,128)(2,1)}, u32[]{:S(2)}, u32[]{:S(2)}) collective-permute-start(bf16[512,384]{1,0:T(8,128)(2,1)} %get-tuple-element.95), channel_id=1, source_target_pairs={{0,2},{2,0},{1,3},{3,1},{4,6},{6,4},{5,7},{7,5},{8,10},{10,8},{9,1... | collective-permute-start | bytes 1179656 | tf_op jit(solution)/shard_map/ppermute | solution.py:258
  367.8 53.4 %collective-permute-start.10 = (bf16[1024,768]{1,0:T(8,128)(2,1)}, bf16[1024,768]{1,0:T(8,128)(2,1)}, u32[]{:S(2)}, u32[]{:S(2)}) collective-permute-start(bf16[1024,768]{1,0:T(8,128)(2,1)} %pad_maximum_fusion.7), channel_id=1, source_target_pairs={{0,1},{1,0},{2,3},{3,2},{4,5},{5,4},{6,7},{7,6},{8,9},{9,8},{10,11... | collective-permute-start | bytes 4718600 | tf_op jit(solution)/shard_map/ppermute | solution.py:267
  410.6 13.5 %collective-permute-start.7 = (bf16[1024,768]{1,0:T(8,128)(2,1)}, bf16[1024,768]{1,0:T(8,128)(2,1)}, u32[]{:S(2)}, u32[]{:S(2)}) collective-permute-start(bf16[1024,768]{1,0:T(8,128)(2,1)} %pad_maximum_fusion.6), channel_id=1, source_target_pairs={{0,1},{1,0},{2,3},{3,2},{4,5},{5,4},{6,7},{7,6},{8,9},{9,8},{10,11... | collective-permute-start | bytes 4718600 | tf_op jit(solution)/shard_map/ppermute | solution.py:267
  443.8 10.4 %slice-start = ((s8[4718592]{0:T(1024)(128)(4,1)}), s8[4194304]{0:T(1024)(128)(4,1)S(1)}, s32[]{:S(2)}) async-start(s8[4718592]{0:T(1024)(128)(4,1)} %bitcast.109), calls=%async_computation.8 | async-start | bytes 8388608
  446.6 7.6 %slice-start.1 = ((s8[4718592]{0:T(1024)(128)(4,1)}), s8[524288]{0:T(1024)(128)(4,1)S(1)}, s32[]{:S(2)}) async-start(s8[4718592]{0:T(1024)(128)(4,1)} %bitcast.109), calls=%async_computation.9 | async-start | bytes 1048576
  470.3 20.4 %collective-permute-start.8 = (bf16[512,768]{1,0:T(8,128)(2,1)S(1)}, bf16[512,768]{1,0:T(8,128)(2,1)S(1)}, u32[]{:S(2)}, u32[]{:S(2)}) collective-permute-start(bf16[512,768]{1,0:T(8,128)(2,1)S(1)} %slice.325), channel_id=1, source_target_pairs={{0,2},{2,0},{1,3},{3,1},{4,6},{6,4},{5,7},{7,5},{8,10},{10,8},{9,1... | collective-permute-start | bytes 2359304 | tf_op jit(solution)/shard_map/ppermute | solution.py:271
  476.2 30.7 %collective-permute-start.11 = (bf16[512,768]{1,0:T(8,128)(2,1)S(1)}, bf16[512,768]{1,0:T(8,128)(2,1)S(1)}, u32[]{:S(2)}, u32[]{:S(2)}) collective-permute-start(bf16[512,768]{1,0:T(8,128)(2,1)S(1)} %slice.324), channel_id=1, source_target_pairs={{0,2},{2,0},{1,3},{3,1},{4,6},{6,4},{5,7},{7,5},{8,10},{10,8},{9,1... | collective-permute-start | bytes 2359304 | tf_op jit(solution)/shard_map/ppermute | solution.py:271
  477.5 13.2 %copy-start.28 = (f32[512,768]{1,0:T(8,128)S(1)}, f32[512,768]{1,0:T(8,128)}, u32[]{:S(2)}) copy-start(f32[512,768]{1,0:T(8,128)} %copy-done.27) | copy-start | bytes 4718596
  478.8 28.1 %copy-start.30 = (f32[512,768]{1,0:T(8,128)S(1)}, f32[512,768]{1,0:T(8,128)}, u32[]{:S(2)}) copy-start(f32[512,768]{1,0:T(8,128)} %copy-done.29) | copy-start | bytes 4718596
  (46 other events, 110.2 us)
Sparse Core Ops, SparseCore 0:
  15.8 89.7 all-gather.3
  109.1 75.2 all-gather.5
  187.2 64.3 all-gather.7
  462.5 169.4 reduce-scatter.3

commit v2 on v1

--- a/solution.py
+++ b/solution.py
@@ -23,7 +23,6 @@
     z=jnp.zeros_like(t)
     return jnp.where(col<HD,t,z), jnp.where(col<HD,z,t)
 
-def dot(a,b): return jnp.dot(a,b,preferred_element_type=f32)
 
 def fwd_kernel(piece, KB, QB, live_ref, q_ref, ko_ref, vo_ref, ks_ref, vs_ref, c_ref, lse_ref,
                kfull, vfull, vT0, vT1, qT0, qT1, acc):
@@ -154,27 +153,289 @@
         cost_estimate=pl.CostEstimate(flops=int(10*nq*L*w*0.6*3),bytes_accessed=12*nq*w*2*2,transcendentals=int(nq*L*w/64*0.6)),
         compiler_params=pltpu.CompilerParams(vmem_limit_bytes=48*2**20,dimension_semantics=("arbitrary",)))(sc,q,kvo,kvo,kvs,kvs,ctx,dctx,lse)
 
-from jax.sharding import PartitionSpec as P
-ALL=("dp","mp")
+NTd=(((1,),(1,)),((),())); TNd=(((0,),(0,)),((),()))
+def dot(a,b): return jnp.dot(a,b,preferred_element_type=f32)
+def dotT(a,b): return lax.dot_general(a,b,NTd,preferred_element_type=f32)
+def Tdot(a,b): return lax.dot_general(a,b,TNd,preferred_element_type=f32)
 epsilon=1e-5
 root_half=0.7071067811865476
 inverse_root_two_pi=0.3989422804014327
 
-def norm_forward(values, gain, shift):
-    center = jnp.mean(values, axis=-1, keepdims=True)
-    offset = values - center
-    inverse = lax.rsqrt(jnp.mean(offset * offset, axis=-1, keepdims=True) + epsilon)
-    normed = offset * inverse
-    return (normed * gain + shift, normed, inverse)
-
-def norm_backward(gradient, normed, inverse, gain):
-    scaled = gradient * gain
-    centered = (scaled - jnp.mean(scaled, axis=-1, keepdims=True)
-        - normed * jnp.mean(scaled * normed, axis=-1, keepdims=True))
-    return (inverse * centered, jnp.sum(gradient * normed, axis=0), jnp.sum(gradient, axis=0))
-
-def dotT(a,b): return lax.dot_general(a,b,(((1,),(1,)),((),())),preferred_element_type=f32)
-def Tdot(a,b): return lax.dot_general(a,b,(((0,),(0,)),((),())),preferred_element_type=f32)
+def ffn_kernel(T, RC, sc_ref, tok_ref, cm_ref, co_ref, cot_ref, wo_ref, win_ref, wout_ref, vec_ref, inb_ref,
+        out_ref, da_ref, dck_ref, dcs_ref, gwo_hbm, gwin_hbm, gwout_hbm, gsm_ref, ginb_ref,
+        gwo, gwin, gwout, n1_s, r1_s, ul_s, acc, db_s, do_s, z_s, sl_s, fb, sem):
+    s=pl.program_id(0); ns=pl.num_programs(0)
+    x=sc_ref[0]
+    rows,D=tok_ref.shape[1:]; FF=win_ref.shape[1]; hw=cm_ref.shape[2]
+    xs=pl.ds(pl.multiple_of(x*hw,hw),hw); ys=pl.ds(pl.multiple_of((1-x)*hw,hw),hw)
+    ob,ag,ash,outb,fg,fs=[vec_ref[i:i+1,:] for i in range(6)]
+    @pl.when(s==0)
+    def _():
+        gsm_ref[...]=jnp.zeros_like(gsm_ref); ginb_ref[...]=jnp.zeros_like(ginb_ref)
+    nr=rows//RC
+    def p1(i,_):
+        r=pl.ds(pl.multiple_of(i*RC,RC),RC)
+        a=tok_ref[0,r,:].astype(f32)+dot(cm_ref[0,r,:],wo_ref[xs,:])+dot(co_ref[0,r,:],wo_ref[ys,:])+ob
+        o=a-jnp.mean(a,axis=-1,keepdims=True)
+        inv=lax.rsqrt(jnp.mean(o*o,axis=-1,keepdims=True)+epsilon)
+        n=o*inv
+        n1_s[r,:]=n; r1_s[r,:]=jnp.broadcast_to(inv,(RC,128))
+        ul_s[r,:]=(n*ag+ash).astype(bf)
+        return 0
+    lax.fori_loop(0,nr,p1,0)
+    nt=FF//T
+    def mm1(t): return dot(ul_s[...],win_ref[:,pl.ds(pl.multiple_of(t*T,T),T)])
+    fb[0]=mm1(0)
+    def p2(t,_):
+        ts=pl.ds(pl.multiple_of(t*T,T),T)
+        @pl.when(t+1<nt)
+        def _(): pass
+        nxt=jnp.minimum(t+1,nt-1)
+        fnext=mm1(nxt)
+        f=fb[lax.rem(t,2)]+inb_ref[:,ts]
+        cdf=0.5*(1.0+lax.erf(f*root_half))
+        pdf=jnp.exp(-0.5*f*f)*inverse_root_two_pi
+        z=(f*cdf).astype(bf)
+        z_s[:,ts]=z; sl_s[:,ts]=(cdf+f*pdf).astype(bf)
+        y=dot(z,wout_ref[ts,:])
+        fb[lax.rem(t+1,2)]=fnext
+        @pl.when(t==0)
+        def _(): acc[...]=y
+        @pl.when(t>0)
+        def _(): acc[...]+=y
+        return 0
+    lax.fori_loop(0,nt,p2,0)
+    def p3(i,_):
+        r=pl.ds(pl.multiple_of(i*RC,RC),RC)
+        b=acc[r,:]+(n1_s[r,:]*ag+ash)+outb
+        o=b-jnp.mean(b,axis=-1,keepdims=True)
+        inv=lax.rsqrt(jnp.mean(o*o,axis=-1,keepdims=True)+epsilon)
+        n=o*inv
+        out_ref[0,r,:]=(n*fg+fs).astype(bf)
+        g=cot_ref[0,r,:].astype(f32)
+        e=g*fg
+        db=inv*(e-jnp.mean(e,axis=-1,keepdims=True)-n*jnp.mean(e*n,axis=-1,keepdims=True))
+        db_s[r,:]=db
+        do=db.astype(bf); do_s[r,:]=do
+        gsm_ref[3:4,:]+=jnp.sum(do.astype(f32),axis=0,keepdims=True)
+        gsm_ref[4:5,:]+=jnp.sum(g*n,axis=0,keepdims=True)
+        gsm_ref[5:6,:]+=jnp.sum(g,axis=0,keepdims=True)
+        return 0
+    lax.fori_loop(0,nr,p3,0)
+    def put(ref,idx,val):
+        @pl.when(s==0)
+        def _(): ref[idx]=val.astype(bf)
+        @pl.when(s>0)
+        def _(): ref[idx]=(ref[idx].astype(f32)+val).astype(bf)
+    def p4(t,_):
+        ts=pl.ds(pl.multiple_of(t*T,T),T)
+        dz=dotT(do_s[...],wout_ref[ts,:])
+        df=(dz*sl_s[:,ts].astype(f32)).astype(bf)
+        put(gwout,(ts,slice(None)),Tdot(z_s[:,ts],do_s[...]))
+        put(gwin,(slice(None),ts),Tdot(ul_s[...],df))
+        y=dotT(df,win_ref[:,ts])
+        ginb_ref[:,ts]+=jnp.sum(df.astype(f32),axis=0,keepdims=True)
+        db_s[...]+=y
+        return 0
+    lax.fori_loop(0,nt,p4,0)
+    @pl.when(s==ns-1)
+    def _():
+        pltpu.make_async_copy(gwin,gwin_hbm,sem.at[0]).start()
+        pltpu.make_async_copy(gwout,gwout_hbm,sem.at[1]).start()
+    def p5(i,_):
+        r=pl.ds(pl.multiple_of(i*RC,RC),RC)
+        du=db_s[r,:]; n=n1_s[r,:]; inv=r1_s[r,0:1]
+        e=du*ag
+        da=inv*(e-jnp.mean(e,axis=-1,keepdims=True)-n*jnp.mean(e*n,axis=-1,keepdims=True))
+        da_ref[0,r,:]=da
+        dm=da.astype(bf); do_s[r,:]=dm
+        gsm_ref[0:1,:]+=jnp.sum(dm.astype(f32),axis=0,keepdims=True)
+        gsm_ref[1:2,:]+=jnp.sum(du*n,axis=0,keepdims=True)
+        gsm_ref[2:3,:]+=jnp.sum(du,axis=0,keepdims=True)
+        dck_ref[0,r,:]=dotT(dm,wo_ref[xs,:]).astype(bf)
+        dcs_ref[0,r,:]=dotT(dm,wo_ref[ys,:]).astype(bf)
+        return 0
+    lax.fori_loop(0,nr,p5,0)
+    put(gwo,(xs,slice(None)),Tdot(cm_ref[0],do_s[...]))
+    put(gwo,(ys,slice(None)),Tdot(co_ref[0],do_s[...]))
+    @pl.when(s==ns-1)
+    def _():
+        pltpu.make_async_copy(gwo,gwo_hbm,sem.at[2]).start()
+        pltpu.make_async_copy(gwin,gwin_hbm,sem.at[0]).wait()
+        pltpu.make_async_copy(gwout,gwout_hbm,sem.at[1]).wait()
+        pltpu.make_async_copy(gwo,gwo_hbm,sem.at[2]).wait()
+
+def ffn(xi, tok, cm, co, cot, wo, win, wout, vec, inb, T=512, RC=128):
+    S,rows,D=tok.shape; FF=win.shape[1]; hw=cm.shape[2]
+    V=pltpu.VMEM
+    slot=lambda w: pl.BlockSpec((1,rows,w),lambda s,p:(s,0,0))
+    full=lambda a: pl.BlockSpec(a.shape,lambda s,p:(0,)*a.ndim,pipeline_mode=pl.Buffered(1))
+    anys=pl.BlockSpec(memory_space=pl.ANY)
+    sd=jax.ShapeDtypeStruct
+    fl=S*rows*D*(2*D+4*FF)*3
+    return pl.pallas_call(functools.partial(ffn_kernel,T,RC),
+        grid_spec=pltpu.PrefetchScalarGridSpec(num_scalar_prefetch=1,grid=(S,),
+            in_specs=[slot(D),slot(hw),slot(hw),slot(D),full(wo),full(win),full(wout),full(vec),full(inb)],
+            out_specs=[slot(D),slot(D),slot(hw),slot(hw),anys,anys,anys,pl.BlockSpec((8,D),lambda s,p:(0,0)),pl.BlockSpec((1,FF),lambda s,p:(0,0))],
+            scratch_shapes=[V((D,D),bf),V((D,FF),bf),V((FF,D),bf),V((rows,D),f32),V((rows,128),f32),V((rows,D),bf),V((rows,D),f32),V((rows,D),f32),V((rows,D),bf),
+                V((rows,FF),bf),V((rows,FF),bf),V((2,rows,T),f32),pltpu.SemaphoreType.DMA((3,))]),
+        out_shape=(sd((S,rows,D),bf),sd((S,rows,D),f32),sd((S,rows,hw),bf),sd((S,rows,hw),bf),sd((D,D),bf),sd((D,FF),bf),sd((FF,D),bf),sd((8,D),f32),sd((1,FF),f32)),
+        name="ffn",
+        cost_estimate=pl.CostEstimate(flops=int(fl),bytes_accessed=40*2**20,transcendentals=2*S*rows*FF),
+        compiler_params=pltpu.CompilerParams(vmem_limit_bytes=62*2**20,dimension_semantics=("arbitrary",)))(xi,tok,cm,co,cot,wo,win,wout,vec,inb)
+
+def qkvb_kernel(last, RC, sc_ref, x_ref, dq_ref, dko_ref, dvo_ref, r_ref, da_ref, w_ref, prev_ref, s_ref, ig_ref, dxo_ref, dw_ref, dqkv, accw):
+    rows,D=x_ref.shape; hw=dq_ref.shape[1]; half=rows//2
+    x=sc_ref[0]
+    for i in range(rows//RC):
+        r=slice(i*RC,(i+1)*RC)
+        dqkv[r,0:hw]=dq_ref[r,:]
+        dqkv[r,hw:2*hw]=(dko_ref[r,:].astype(f32)+r_ref[r,0:hw].astype(f32)).astype(bf)
+        dqkv[r,2*hw:3*hw]=(dvo_ref[r,:].astype(f32)+r_ref[r,hw:2*hw].astype(f32)).astype(bf)
+    for i in range(rows//RC):
+        r=slice(i*RC,(i+1)*RC)
+        dx=dotT(dqkv[r,:],w_ref[:,0:3*hw])
+        if i*RC<half: ig_ref[r,:]=da_ref[r,:]+dx
+        else: dxo_ref[i*RC-half:(i+1)*RC-half,:]=dx.astype(bf)
+    W=3*hw
+    for j in range(3):
+        cs=slice(j*hw,(j+1)*hw)
+        v=Tdot(x_ref[...],dqkv[:,cs])+prev_ref[:,cs]
+        dw_ref[:,cs]=v.astype(dw_ref.dtype)
+    ones=jnp.ones((rows,128),bf)
+    col=lax.broadcasted_iota(jnp.int32,(hw,128),1)
+    b=jnp.where(col==0,Tdot(dqkv[:,0:hw],ones),0.0)+jnp.where(col==1,Tdot(dqkv[:,2*hw:],ones),0.0)
+    xs=pl.ds(pl.multiple_of(x*hw,hw),hw)
+    if last:
+        accw[...]=prev_ref[:,W:]+jnp.transpose(s_ref[...])
+        accw[xs,:]+=b
+        dw_ref[:,W:]=accw[...].astype(bf)
+    else:
+        dw_ref[:,W:]=jnp.zeros_like(accw)
+        dw_ref[xs,W:]=b
+
+def qkvb(last, xi, X, dq, dko, dvo, r, da, w, prev, small, RC=256):
+    rows,D=X.shape; hw=dq.shape[1]; W=3*hw+128
+    sd=jax.ShapeDtypeStruct; V=pltpu.VMEM
+    vm=pl.BlockSpec(memory_space=pltpu.VMEM)
+    return pl.pallas_call(functools.partial(qkvb_kernel,last,RC),
+        grid_spec=pltpu.PrefetchScalarGridSpec(num_scalar_prefetch=1,grid=(),in_specs=[vm]*9,out_specs=[vm]*3,
+            scratch_shapes=[V((rows,3*hw),bf),V((D,128),f32)]),
+        out_shape=(sd((rows//2,D),f32),sd((rows//2,D),bf),sd((D,W),bf if last else f32)),
+        name="qkvb_last" if last else "qkvb",
+        cost_estimate=pl.CostEstimate(flops=4*rows*D*3*hw,bytes_accessed=20*2**20,transcendentals=0),
+        compiler_params=pltpu.CompilerParams(vmem_limit_bytes=48*2**20))(xi,X,dq,dko,dvo,r,da,w,prev,small)
+
+MESH=pl.DeviceIdType.MESH
+def reduce_kernel(Z, gin, gout, go, gq, dxo, o_in, o_out, o_o, o_q, o_k, o_v, o_s, rx,
+        a1,a2,a3,a4, c1,c2,c3,c4, p1,p2,p3,p4, u1,u2,u3, f1,f2,f3,f4, xb, xr, lsem, ssem, rsem):
+    g=lax.axis_index("dp"); m=lax.axis_index("mp")
+    h=g//2; y=lax.rem(g,2); x=m//2; c=lax.rem(m,2)
+    core={"dp":g,"mp":2*x+1-c}; xn={"dp":g,"mp":2*(1-x)+c}; yn={"dp":2*h+1-y,"mp":m}
+    zz=[lax.rem(h+1+t,Z) for t in range(Z)]
+    zn=[{"dp":2*zz[t]+y,"mp":m} for t in range(Z)]
+    bar=pltpu.get_barrier_semaphore()
+    def greet(dev): pl.semaphore_signal(bar,inc=1,device_id=dev,device_id_type=MESH)
+    greet(core); greet(xn); greet(yn)
+    for t in range(Z-1): greet(zn[t])
+    pl.semaphore_wait(bar,3+Z-1)
+    A=[a1,a2,a3,a4]; C=[c1,c2,c3,c4]; Pb=[p1,p2,p3,p4]; U=[u1,u2,u3]; F=[f1,f2,f3,f4]; G=[gin,gout,go,gq]
+    def rc(src,dst,a,s,t,dev):
+        return pltpu.make_async_remote_copy(src_ref=src,dst_ref=dst,send_sem=ssem.at[a,s,t],recv_sem=rsem.at[a,s,t],device_id=dev,device_id_type=MESH)
+    pend=[]
+    def go_(d): d.start(); pend.append(d); return d
+    xd=rc(dxo,rx,0,4,0,xn)
+    order=[3,0,1,2]
+    core_d={}; loc={}
+    for t in range(Z):
+        for a in order:
+            d=rc(G[a].at[zz[t],:,:,1-c],C[a].at[t],a,0,t,core); d.start(); core_d[a,t]=d
+            l=pltpu.make_async_copy(G[a].at[zz[t],:,:,c],A[a].at[t],lsem.at[a,t]); l.start(); loc[a,t]=l
+        if t==0: xd.start()
+    def add(ref,idx,other):
+        ref[idx]=(ref[idx].astype(f32)+other.astype(f32)).astype(bf)
+    s1={};s2={};s3={}
+    def stage0(t):
+        for a in order:
+            loc[a,t].wait(); core_d[a,t].wait_recv()
+            A[a][t]=(A[a][t].astype(f32)+C[a][t].astype(f32)).astype(bf)
+            if a==0: d=rc(A[a].at[t,:,1-x],Pb[a].at[t],a,1,t,xn)
+            else: d=rc(A[a].at[t,1-y],Pb[a].at[t],a,1,t,yn)
+            d.start(); s1[a,t]=d
+    def stage1(t):
+        for a in order:
+            s1[a,t].wait_recv()
+            if a==0:
+                for k in range(2): add(A[a],(t,k,x),Pb[a][t,k])
+                d=rc(A[a].at[t,1-y,x],U[a].at[t],a,2,t,yn)
+            else:
+                for k in range(2): add(A[a],(t,y,k),Pb[a][t,k])
+                if a==3:
+                    if t<Z-1:
+                        d=rc(A[a].at[t,y],F[a].at[t],a,3,t,zn[t])
+                    else: d=None
+                else: d=rc(A[a].at[t,y,1-x],U[a].at[t],a,2,t,xn)
+            if d is not None:
+                d.start()
+                if a==3: s3[a,t]=d
+                else: s2[a,t]=d
+    def stage2(t):
+        for a in (0,1,2):
+            s2[a,t].wait_recv()
+            add(A[a],(t,y,x),U[a][t])
+            if t<Z-1:
+                d=rc(A[a].at[t,y,x],F[a].at[t],a,3,t,zn[t]); d.start(); s3[a,t]=d
+    for t in range(Z+2):
+        if t<Z: stage0(t)
+        if 0<=t-1<Z: stage1(t-1)
+        if 0<=t-2<Z: stage2(t-2)
+    for t in range(Z-1): s3[3,t].wait_recv()
+    hw=(gq.shape[-1]-128)//3
+    def fin4(k):
+        v=a4[Z-1,y,k].astype(f32)
+        for t in range(Z-1): v=v+f4[t,k].astype(f32)
+        return v
+    xb[...]=fin4(1-x).astype(bf)
+    xd4=rc(xb,xr,3,2,0,xn); xd4.start()
+    for a,o in ((0,o_in),(1,o_out),(2,o_o)):
+        v=A[a][Z-1,y,x].astype(f32)
+        for t in range(Z-1):
+            s3[a,t].wait_recv(); v=v+F[a][t].astype(f32)
+        o[...]=v
+    mine=fin4(x)
+    xs=pl.ds(pl.multiple_of(x*hw,hw),hw); ys=pl.ds(pl.multiple_of((1-x)*hw,hw),hw)
+    xd4.wait_recv()
+    for i,o in enumerate((o_q,o_k,o_v)):
+        o[:,xs]=mine[:,i*hw:(i+1)*hw]
+        o[:,ys]=xr[:,i*hw:(i+1)*hw].astype(f32)
+    o_s[...]=mine[:,3*hw:]+xr[:,3*hw:].astype(f32)
+    xd.wait()
+    xd4.wait_send()
+    for dd in (core_d,s1,s2,s3):
+        for d in dd.values(): d.wait_send()
+
+def reduce_grads(G, gin, gout, go, gq, dxo):
+    Z=G//2
+    n=4*G
+    sd=jax.ShapeDtypeStruct; V=pltpu.VMEM
+    arrs=[]
+    for a in (gin,gout,go,gq):
+        arrs.append(a.reshape(Z,2,2,2,a.shape[0]//n,a.shape[1]))
+    rw=[(a.shape[4],a.shape[5]) for a in arrs]
+    D=go.shape[1]
+    anys=pl.BlockSpec(memory_space=pl.ANY); vm=pl.BlockSpec(memory_space=pltpu.VMEM)
+    scr=[V((Z,2,2)+s,bf) for s in rw]+[V((Z,2,2)+s,bf) for s in rw]+[V((Z,2)+s,bf) for s in rw]+[V((Z,)+s,bf) for s in rw[:3]]
+    scr+=[V((Z,)+s,bf) for s in rw[:3]]+[V((Z,2)+rw[3],bf)]+[V(rw[3],bf)]*2
+    scr+=[pltpu.SemaphoreType.DMA((4,Z)),pltpu.SemaphoreType.DMA((4,5,Z)),pltpu.SemaphoreType.DMA((4,5,Z))]
+    return pl.pallas_call(functools.partial(reduce_kernel,Z),
+        in_specs=[anys]*5,out_specs=[vm]*7+[anys],
+        out_shape=tuple(sd(s,f32) for s in rw[:3])+tuple(sd((rw[2][0],D),f32) for _ in range(3))+(sd((rw[2][0],128),f32),sd(dxo.shape,bf)),
+        scratch_shapes=scr,name="reduce_grads",
+        cost_estimate=pl.CostEstimate(flops=10**7,bytes_accessed=30*2**20,transcendentals=0),
+        compiler_params=pltpu.CompilerParams(vmem_limit_bytes=62*2**20,collective_id=1,has_side_effects=True))(*arrs,dxo)
+
+from jax.sharding import PartitionSpec as P
+ALL=("dp","mp")
 
 XP=[(0,2),(2,0),(1,3),(3,1)]
 CP=[(0,1),(1,0),(2,3),(3,2)]
@@ -202,6 +463,9 @@
     inb = smalls[8:8+FF//D].reshape(FF//D,n,sh).transpose(1,0,2).reshape(FF).astype(f32)
     cut = lambda i: lax.dynamic_slice(qkv,(0,i*D+x*hw),(D,hw))
     wq,wk,wv = cut(0),cut(1),cut(2)
+    wx = jnp.concatenate([wq,wk,wv],axis=1)
+    xi = x.reshape(1).astype(jnp.int32)
+    vec = jnp.stack([ob,ag,ash,outb,fg,fs,ob,ob])
     qbx = lax.dynamic_slice(qb,(x*hw,),(hw,)); vbx = lax.dynamic_slice(vb,(x*hw,),(hw,))
     R = rows//G
     mixed = lax.all_to_all(tokens.reshape(micro,G,R,D),"dp",split_axis=1,concat_axis=0,tiled=True).reshape(micro*G,R,D)
@@ -223,69 +487,27 @@
         ctx,lse = attn_fwd(q,kvo,kvs,sc,rows)
         c_oth = lax.ppermute(ctx[rows:],"mp",XP)
         st.append([own,X,sc,q,kvo,kvs,ctx,lse,c_oth])
-    dW=None
-    st2=[]
+    own2 = jnp.stack([t[0] for t in st])
+    cm = jnp.stack([t[6][:rows] for t in st]); co = jnp.stack([t[8] for t in st])
+    out,dA,dck,dcs,gwo,gwin,gwout,gsm,ginb = ffn(xi,own2,cm,co,cotangent,w_o,w_in,w_out,vec,inb.reshape(1,FF))
+    small_g = jnp.concatenate([jnp.zeros((2,D),f32),gsm[:6],ginb.reshape(n,FF//D,sh).transpose(1,0,2).reshape(FF//D,D),jnp.zeros((128-8-FF//D,D),f32)],axis=0)
+    prev = jnp.zeros((D,3*hw+128),f32)
+    igs=[]
+    got = [lax.ppermute(dcs[s],"mp",XP) for s in range(micro)]
     for s in range(micro):
         own,X,sc,q,kvo,kvs,ctx,lse,c_oth = st[s]
-        mine = ctx[:rows]
-        cfull = jnp.where(x==0,jnp.concatenate([mine,c_oth],axis=1),jnp.concatenate([c_oth,mine],axis=1))
-        A = own.astype(f32)+jnp.dot(cfull,w_o,preferred_element_type=f32)+ob
-        U,n1,r1 = norm_forward(A,ag,ash)
-        ul = U.astype(bf)
-        F = jnp.dot(ul,w_in,preferred_element_type=f32)+inb
-        Z = jax.nn.gelu(F,approximate=False).astype(bf)
-        B = U+jnp.dot(Z,w_out,preferred_element_type=f32)+outb
-        out,n2,r2 = norm_forward(B,fg,fs)
-        outs.append(out.astype(bf))
-        G_ = cotangent[s].astype(f32)
-        dB,dfg,dfs = norm_backward(G_,n2,r2,fg)
-        dO = dB.astype(bf)
-        doutb = jnp.sum(dO.astype(f32),axis=0)
-        dwout = Tdot(Z,dO)
-        dZ = dotT(dO,w_out)
-        slope = 0.5*(1.0+lax.erf(F*root_half))+F*jnp.exp(-0.5*F*F)*inverse_root_two_pi
-        dF = (dZ*slope).astype(bf)
-        dinb = jnp.sum(dF.astype(f32),axis=0)
-        dwin = Tdot(ul,dF)
-        dU = dB+dotT(dF,w_in)
-        dA,dag,dash = norm_backward(dU,n1,r1,ag)
-        dM = dA.astype(bf)
-        dob = jnp.sum(dM.astype(f32),axis=0)
-        dwo = Tdot(cfull,dM)
-        dC = dotT(dM,w_o).astype(bf)
-        dc_l,dc_r = dC[:,:hw],dC[:,hw:]
-        keep = jnp.where(x==0,dc_l,dc_r); send = jnp.where(x==0,dc_r,dc_l)
-        got = lax.ppermute(send,"mp",XP)
-        st2.append((dA,jnp.concatenate([keep,got],axis=0)))
-        now = [dwo,dwin,dwout,dob,dag,dash,doutb,dfg,dfs,dinb]
-        dW = now if dW is None else [a+b for a,b in zip(dW,now)]
-    dQKV=None
-    for s in range(micro):
-        own,X,sc,q,kvo,kvs,ctx,lse,c_oth = st[s]
-        dA,dctx = st2[s]
+        dctx = jnp.concatenate([dck[s],got[s]],axis=0)
         dq,dko,dvo,dks,dvs = attn_bwd(q,kvo,kvs,ctx,dctx,lse,sc,rows)
         r_ = lax.ppermute(jnp.concatenate([dks,dvs],axis=1),"mp",CP)
-        dk = (dko.astype(f32)+r_[:,:hw].astype(f32)).astype(bf)
-        dv = (dvo.astype(f32)+r_[:,hw:].astype(f32)).astype(bf)
-        dXp = dotT(dq,wq)+dotT(dk,wk)+dotT(dv,wv)
-        rx = lax.ppermute(dXp[rows:].astype(bf),"mp",XP)
-        igs.append(dA+dXp[:rows]+rx.astype(f32))
-        now = [Tdot(X,dq),Tdot(X,dk),Tdot(X,dv),jnp.sum(dq.astype(f32),axis=0),jnp.sum(dv.astype(f32),axis=0)]
-        dQKV = now if dQKV is None else [a+b for a,b in zip(dQKV,now)]
-    wide = lambda t: lax.dynamic_update_slice(jnp.zeros(t.shape[:-1]+(D,),bf),t.astype(bf),(0,)*(t.ndim-1)+(x*hw,))
-    dwq,dwk,dwv,dqb,dvb = [wide(t) for t in dQKV]
-    dwo,dwin,dwout,dob,dag,dash,doutb,dfg,dfs,dinb = [t.astype(bf) for t in dW]
-    dsm = jnp.concatenate([jnp.stack([dqb,dvb,dob,dag,dash,doutb,dfg,dfs]),
-        dinb.reshape(n,FF//D,sh).transpose(1,0,2).reshape(FF//D,D), jnp.zeros((128-8-FF//D,D),bf)],axis=0)
-    dwo2 = dwout.reshape(n,FF//D,sh,D).transpose(0,2,1,3).reshape(D,FF)
-    big = jnp.concatenate([dwq,dwk,dwv,dwo,dwin,dwo2,jnp.transpose(dsm)],axis=1)
-    red = lax.psum_scatter(big,ALL,scatter_dimension=0,tiled=True).astype(f32)
-    pick = lambda i: red[:,i*D:(i+1)*D]
-    gin = red[:,4*D:4*D+FF]
-    gout = red[:,4*D+FF:4*D+2*FF].reshape(sh,FF//D,D).transpose(1,0,2).reshape(sh*(FF//D),D)
-    sm = jnp.transpose(red[:,4*D+2*FF:])
-    ginb = sm[8:8+FF//D].reshape(-1)
-    return (jnp.stack(outs),jnp.stack(igs),pick(0),pick(1),pick(2),pick(3),sm[0],sm[1],sm[2],sm[3],sm[4],gin,ginb,gout,sm[5],sm[6],sm[7])
+        last = s==micro-1
+        ig,dxo,prev = qkvb(last,xi,X,dq,dko,dvo,r_,dA[s],wx,prev,small_g)
+        igs.append((ig,dxo))
+    rxa = lax.ppermute(igs[0][1],"mp",XP)
+    gin,gout,go,gq,gk,gv,gs,rxb = reduce_grads(G,gwin,gwout,gwo,prev,igs[1][1])
+    ig = jnp.stack([igs[0][0]+rxa.astype(f32),igs[1][0]+rxb.astype(f32)])
+    sm = jnp.transpose(gs)
+    ginb_o = sm[8:8+FF//D].reshape(-1)
+    return (out,ig,gq,gk,gv,go,sm[0],sm[1],sm[2],sm[3],sm[4],gin,ginb_o,gout,sm[5],sm[6],sm[7])
 
 def solution(mesh):
     r2=P(ALL,None); r1=P(ALL); t=P("dp","mp",None)

time: 651 us -> 552 us (0.85)
  Pallas kernels: 89.7 us -> 273 us
  matrix products: 148 us -> 12.3 us
  waiting for transfers between devices: 240 us -> 110 us
  local copies, waits for them, and re-layouts: 68.3 us -> 50.5 us
    pallas_call x0 -> x4, Pallas kernels: none -> 177 us  [the longest x1 79.8 us: reduce_grads(): pl.pallas_call(functools.partial(reduce_kernel, Z), in_specs=[anys] * 5,...]
    dot_general x30 -> x0, matrix products: 133 us -> none  [the longest x12 45.1 us: Tdot(): lax.dot_general(a, b, (((0,), (0,)), ((), ())), preferred_element_type=f32)]
    unnamed x5 -> x3, waiting for transfers between devices: 123 us -> 0.71 us
    ppermute x4 -> x3, waiting for transfers between devices: 27.8 us -> 9.78 us  [the longest x2 9.77 us: on_device(): got = [lax.ppermute(dcs[s], 'mp', XP) for s in range(micro)]]
    convert_element_type x11 -> x0, local copies, waits for them, and re-layouts: 14.1 us -> none  [on_device(): t.astype(bf)]
    ppermute x2, waiting for transfers between devices: 8.64 us -> 18.7 us  [on_device(): c_oth = lax.ppermute(ctx[rows:], 'mp', XP)]
    reduce_sum x12 -> x0, other arithmetic: 9.17 us -> none  [the longest x2 2.93 us: on_device(): jnp.sum(dv.astype(f32), axis=0)]
    unnamed x158 -> x92, local copies, waits for them, and re-layouts: 19.8 us -> 10.7 us
  transfers between devices with their start and end apart: 18 -> 16, of which waited for: 7 -> 6; matrix products, arithmetic and copies ran while one was open for 20% -> 12% of each run, Pallas kernels for 14% -> 36%
where the time goes in v2:
time: 552 us; the launch traced here: 543 us
  Pallas kernels  273 us (49%)
  waiting for transfers between devices  110 us (20%)
  local copies, waits for them, and re-layouts  50.5 us (9%)
  blocking collectives  33.2 us (6%)
  other arithmetic  28 us (5%)
  starting transfers between devices  21.3 us (4%)
  between operations  14.8 us (3%)
  matrix products  12.3 us (2%)
    pallas_call x1, Pallas kernels, reduce_grads(): pl.pallas_call(functools.partial(reduce_kernel, Z), in_specs=[anys] * 5,...  79.8 us
    pallas_call x1, Pallas kernels, ffn(): pl.pallas_call(functools.partial(ffn_kernel, T, RC), grid_spec=pltpu.Pref...  75.3 us
    pallas_call x2, Pallas kernels, attn_bwd(): pl.pallas_call(functools.partial(bwd_kernel, piece, KB, QB), grid_spec=pl...  57.4 us
    all_to_all x1, waiting for transfers between devices, on_device(): lax.all_to_all(tokens.reshape(micro, G, R, D), 'dp', split_axis=1, concat...  42.9 us
    pallas_call x2, Pallas kernels, attn_fwd(): pl.pallas_call(functools.partial(fwd_kernel, piece, KB, QB), grid_spec=pl...  38.3 us
    all_to_all x1, blocking collectives, on_device(): lax.all_to_all(picked[:, s], 'dp', split_axis=0, concat_axis=0, tiled=True)  33.2 us
    all_to_all x1, waiting for transfers between devices, on_device(): lax.all_to_all(picked[:, s], 'dp', split_axis=0, concat_axis=0, tiled=True)  22.8 us
    pallas_call x2, Pallas kernels, qkvb(): pl.pallas_call(functools.partial(qkvb_kernel, last, RC), grid_spec=pltpu....  21.8 us
  transfers between devices with their start and end apart: 16, of which 6 were waited for; matrix products, arithmetic and copies ran while one was open for 12% of the time, Pallas kernels for 36%

profile of v2, /device:TPU:0, one launch (start us, length us, event | category | flops | bytes accessed | tf_op | source)
XLA Modules:
  0.0 543.2 jit_solution(14032024982050602729)
XLA Ops:
  14.1 1.6 concatenate.37
  15.7 1.6 pad_maximum_fusion.13
  17.3 2.7 copy.89
  20.0 7.4 %all-to-all-start = ((bf16[2,8,64,768]{3,2,0,1:T(8,128)(2,1)}), bf16[2,8,64,768]{3,2,0,1:T(8,128)(2,1)S(1)}, u32[]{:S(2)}, u32[]{:S(2)}) async-start(bf16[2,8,64,768]{3,2,0,1:T(8,128)(2,1)} %copy.89), calls=%async_computation | async-start | bytes 3145728 | tf_op jit(solution)/shard_map/all_to_all | solution.py:471
  29.0 42.9 %all-to-all-done = bf16[2,8,64,768]{3,2,0,1:T(8,128)(2,1)S(1)} async-done(((bf16[2,8,64,768]{3,2,0,1:T(8,128)(2,1)}), bf16[2,8,64,768]{3,2,0,1:T(8,128)(2,1)S(1)}, u32[]{:S(2)}, u32[]{:S(2)}) %all-to-all-start) | async-done | bytes 1572896 | tf_op jit(solution)/shard_map/all_to_all | solution.py:471
  73.8 33.2 %all_to_all.25 = bf16[8,64,768]{2,1,0:T(8,128)(2,1)S(1)} all-to-all(bf16[8,64,768]{2,1,0:T(8,128)(2,1)S(1)} %get-tuple-element.107), channel_id=1, replica_groups=mesh['dp'=8,'mp'=4] {'dp'}, dimensions={0} | all-to-all | bytes 1572864 | tf_op jit(solution)/shard_map/all_to_all | solution.py:477
  107.0 4.2 all-to-all-start.1
  111.2 1.5 collective-permute-start.2
  112.8 22.8 %all-to-all-done.1 = bf16[8,64,768]{2,1,0:T(8,128)(2,1)} async-done(((bf16[8,64,768]{2,1,0:T(8,128)(2,1)}), bf16[8,64,768]{2,1,0:T(8,128)(2,1)}, u32[]{:S(2)}, u32[]{:S(2)}) %all-to-all-start.1) | async-done | bytes 786464 | tf_op jit(solution)/shard_map/all_to_all | solution.py:477
  135.6 1.5 collective-permute-start
  139.0 2.5 constant_dynamic-slice_fusion.1
  143.7 15.6 %collective-permute-done = bf16[512,768]{1,0:T(8,128)(2,1)} collective-permute-done((bf16[512,768]{1,0:T(8,128)(2,1)}, bf16[512,768]{1,0:T(8,128)(2,1)}, u32[]{:S(2)}, u32[]{:S(2)}) %collective-permute-start) | collective-permute-done | bytes 786464 | tf_op jit(solution)/shard_map/ppermute | solution.py:478
  159.3 2.7 convolution_convert_fusion.1
  162.0 2.4 add_convert_fusion.2
  164.4 1.4 pad_maximum_fusion.4.ko_ref.vo_ref
  168.8 2.6 add_convert_fusion.1.q_ref
  171.4 2.6 add_convert_fusion.3.q_ref
  174.1 1.2 copy-done.5
  175.2 1.4 copy-done.6
  176.6 11.5 %attn_fwd.3 = (bf16[1024,384]{1,0:T(8,128)(2,1)S(1)}, f32[3,2,1024]{2,1,0:T(2,128)S(1)}) custom-call(s32[3]{0:T(128)S(1)} %add_add_fusion.1.live_ref, bf16[1024,384]{1,0:T(8,128)(2,1)S(1)} %add_convert_fusion.1.q_ref, bf16[1024,768]{1,0:T(8,128)(2,1)S(1)} %pad_maximum_fusion.6.ko_ref.vo_ref, bf16[1024,768]{1,0:T(8,128)(2,1)S(1)} %pad_maximum_fusion.6.ko_ref.vo_ref, ...), custom_call_target="tpu_custom_call" | custom-call | flops 5798205952 | bytes 9437184 | tf_op jit(solution)/shard_map/attn_fwd/pallas_call | solution.py:70
  188.2 26.8 %attn_fwd.2 = (bf16[1024,384]{1,0:T(8,128)(2,1)S(1)}, f32[3,2,1024]{2,1,0:T(2,128)S(1)}) custom-call(s32[3]{0:T(128)S(1)} %add_add_fusion.live_ref, bf16[1024,384]{1,0:T(8,128)(2,1)S(1)} %add_convert_fusion.3.q_ref, bf16[1024,768]{1,0:T(8,128)(2,1)} %pad_maximum_fusion.4.ko_ref.vo_ref, bf16[1024,768]{1,0:T(8,128)(2,1)} %pad_maximum_fusion.4.ko_ref.vo_ref, ...), custom_call_target="tpu_custom_call" | custom-call | flops 5798205952 | bytes 9437184 | tf_op jit(solution)/shard_map/attn_fwd/pallas_call | solution.py:70
  218.9 2.5 pad_maximum_fusion.2.tok_ref
  224.6 4.5 collective-permute-done.4
  229.1 14.2 %collective-permute-done.5 = bf16[512,384]{1,0:T(8,128)(2,1)} collective-permute-done((bf16[512,384]{1,0:T(8,128)(2,1)}, bf16[512,384]{1,0:T(8,128)(2,1)}, u32[]{:S(2)}, u32[]{:S(2)}) %collective-permute-start.5) | collective-permute-done | bytes 393248 | tf_op jit(solution)/shard_map/ppermute | solution.py:488
  243.3 2.1 pad_maximum_fusion.10.co_ref
  245.4 4.9 slice.135.win_ref
  250.3 2.4 slice.134.wo_ref
  252.7 75.3 %ffn.1 = (bf16[2,512,768]{2,1,0:T(8,128)(2,1)}, f32[2,512,768]{2,1,0:T(8,128)}, bf16[2,512,384]{2,1,0:T(8,128)(2,1)}, bf16[2,512,384]{2,1,0:T(8,128)(2,1)}, bf16...) custom-call(s32[1]{0:T(128)} %bitcast.sc_ref, ...), custom_call_target="tpu_custom_call" | custom-call | flops 32614907904 | bytes 41943040 | tf_op jit(solution)/shard_map/ffn/pallas_call | solution.py:276
  328.1 1.3 slice_bitcast_fusion.6
  329.4 2.1 collective-permute-start.6
  331.6 9.8 %collective-permute-done.6 = bf16[512,384]{1,0:T(8,128)(2,1)S(1)} collective-permute-done((bf16[512,384]{1,0:T(8,128)(2,1)S(1)}, bf16[512,384]{1,0:T(8,128)(2,1)S(1)}, u32[]{:S(2)}, u32[]{:S(2)}) %collective-permute-start.6) | collective-permute-done | bytes 393248 | tf_op jit(solution)/shard_map/ppermute | solution.py:496
  342.4 39.0 %attn_bwd.2 = (bf16[1024,384]{1,0:T(8,128)(2,1)S(1)}, bf16[1024,384]{1,0:T(8,128)(2,1)S(1)}, bf16[1024,384]{1,0:T(8,128)(2,1)S(1)}, bf16[1024,384]{1,0:T(8,128)(2,1)S(1)}, bf16[1024,384]{1,0:T(8,128)(2,1)S(1)}) custom-call(s32[3]{0:T(128)S(1)} %add_add_fusion.live_ref, bf16[1024,384]{1,0:T(8,128)(2,1)S(1)} %copy-done.20, ...), custom_call_target="tpu_custom_call" | custom-call | flops 14495514624 | bytes 18874368 | tf_op jit(solution)/shard_map/attn_bwd/pallas_call | solution.py:146
  381.4 1.4 pad_maximum_fusion.7
  384.4 18.4 %attn_bwd.3 = (bf16[1024,384]{1,0:T(8,128)(2,1)S(1)}, bf16[1024,384]{1,0:T(8,128)(2,1)S(1)}, bf16[1024,384]{1,0:T(8,128)(2,1)S(1)}, bf16[1024,384]{1,0:T(8,128)(2,1)S(1)}, bf16[1024,384]{1,0:T(8,128)(2,1)S(1)}) custom-call(s32[3]{0:T(128)S(1)} %add_add_fusion.1.live_ref, bf16[1024,384]{1,0:T(8,128)(2,1)S(1)} %copy-done.18, bf16[1024,768]{1,0:T(8,128)(2,1)} %copy-done.2, ...), custom_call_target="tpu_custom_call" | custom-call | flops 14495514624 | bytes 18874368 | tf_op jit(solution)/shard_map/attn_bwd/pallas_call | solution.py:146
  402.8 1.4 pad_maximum_fusion.8
  404.9 2.8 pad_maximum_fusion.3.x_ref
  407.7 1.4 pad_maximum_fusion.1.w_ref
  410.6 3.9 slice_bitcast_fusion.1
  414.5 2.2 broadcast_in_dim.37.prev_ref
  416.7 11.3 %qkvb.1 = (f32[512,768]{1,0:T(8,128)S(1)}, bf16[512,768]{1,0:T(8,128)(2,1)}, f32[768,1280]{1,0:T(8,128)}) custom-call(s32[1]{0:T(128)} %bitcast.sc_ref, bf16[1024,768]{1,0:T(8,128)(2,1)} %pad_maximum_fusion.3.x_ref, bf16[1024,384]{1,0:T(8,128)(2,1)S(1)} %get-tuple-element.60.dq_ref, bf16[1024,384]{1,0:T(8,128)(2,1)S(1)} %copy-done.8, ...), custom_call_target="tpu_custom_call" | custom-call | flops 3623878656 | bytes 20971520 | tf_op jit(solution)/shard_map/qkvb/pallas_call | solution.py:321
  428.0 2.2 collective-permute-start.8
  430.2 1.3 pad_maximum_fusion.5.x_ref
  431.5 10.5 %qkvb_last.1 = (f32[512,768]{1,0:T(8,128)S(1)}, bf16[512,768]{1,0:T(8,128)(2,1)S(1)}, bf16[768,1280]{1,0:T(8,128)(2,1)}) custom-call(s32[1]{0:T(128)} %bitcast.sc_ref, bf16[1024,768]{1,0:T(8,128)(2,1)} %pad_maximum_fusion.5.x_ref, bf16[1024,384]{1,0:T(8,128)(2,1)S(1)} %copy-done.12, bf16[1024,384]{1,0:T(8,128)(2,1)S(1)} %copy-done.14, ...), custom_call_target="tpu_custom_call" | custom-call | flops 3623878656 | bytes 20971520 | tf_op jit(solution)/shard_map/qkvb_last/pallas_call | solution.py:321
  444.1 79.8 %reduce_grads.1 = (f32[24,3072]{1,0:T(8,128)}, f32[96,768]{1,0:T(8,128)}, f32[24,768]{1,0:T(8,128)}, f32[24,768]{1,0:T(8,128)}, f32[24,768]{1,0:T(8,128)}, /*ind...) custom-call(bf16[4,2,2,2,24,3072]{5,4,3,2,1,0:T(8,128)(2,1)} %bitcast.74, ...), custom_call_target="tpu_custom_call" | custom-call | flops 10000000 | bytes 31457280 | tf_op jit(solution)/shard_map/reduce_grads/pallas_call | solution.py:430
  525.3 1.8 slice_reduce_fusion
  527.1 1.8 add_bitcast_fusion
  528.9 1.3 add_bitcast_fusion.1
  530.3 1.9 pad_maximum_fusion
  (167 shorter events, 37.0 us)
Async XLA Ops:
  7.2 21.0 %copy-start = (s32[16]{0:T(128)S(1)}, s32[16]{0:T(128)}, u32[]{:S(2)}) copy-start(s32[16]{0:T(128)} %param.20) | copy-start | bytes 196
  7.2 129.8 %all-gather.4.cloned.1.call-start = ((), (), s32[]{:S(2)}) async-start(), calls=%async_computation.3 | async-start | bytes 3852288 | tf_op jit(solution)/shard_map/all_gather | solution.py:457
  15.7 229.7 %all-gather.6.cloned.1.call-start = ((), (), s32[]{:S(2)}) async-start(), calls=%async_computation.4 | async-start | bytes 6082560 | tf_op jit(solution)/shard_map/all_gather | solution.py:458
  20.0 8.2 %copy-start.42 = (s32[16]{0:T(128)S(1)}, s32[16]{0:T(128)}, u32[]{:S(2)}) copy-start(s32[16]{0:T(128)} %param.21) | copy-start | bytes 196
  20.0 51.9 %all-to-all-start = ((bf16[2,8,64,768]{3,2,0,1:T(8,128)(2,1)}), bf16[2,8,64,768]{3,2,0,1:T(8,128)(2,1)S(1)}, u32[]{:S(2)}, u32[]{:S(2)}) async-start(bf16[2,8,64,768]{3,2,0,1:T(8,128)(2,1)} %copy.89), calls=%async_computation | async-start | bytes 3145728 | tf_op jit(solution)/shard_map/all_to_all | solution.py:471
  27.4 225.3 %all-gather.8.cloned.1.call-start = ((), (), s32[]{:S(2)}) async-start(), calls=%async_computation.5 | async-start | bytes 4866048 | tf_op jit(solution)/shard_map/all_gather | solution.py:459
  107.0 35.4 %copy-start.21 = (bf16[8,64,768]{2,1,0:T(8,128)(2,1)}, bf16[8,64,768]{2,1,0:T(8,128)(2,1)S(1)}, u32[]{:S(2)}) copy-start(bf16[8,64,768]{2,1,0:T(8,128)(2,1)S(1)} %all_to_all.25) | copy-start | bytes 2359300
  107.0 28.6 %all-to-all-start.1 = ((bf16[8,64,768]{2,1,0:T(8,128)(2,1)}), bf16[8,64,768]{2,1,0:T(8,128)(2,1)}, u32[]{:S(2)}, u32[]{:S(2)}) async-start(bf16[8,64,768]{2,1,0:T(8,128)(2,1)} %get-tuple-element.106), calls=%async_computation.1 | async-start | bytes 1572864 | tf_op jit(solution)/shard_map/all_to_all | solution.py:477
  111.2 30.2 %collective-permute-start.2 = (bf16[512,768]{1,0:T(8,128)(2,1)S(1)}, bf16[512,768]{1,0:T(8,128)(2,1)S(1)}, u32[]{:S(2)}, u32[]{:S(2)}) collective-permute-start(bf16[512,768]{1,0:T(8,128)(2,1)S(1)} %bitcast.66), channel_id=1, source_target_pairs={{0,2},{2,0},{1,3},{3,1},{4,6},{6,4},{5,7},{7,5},{8,10},{10,8},{9,1... | collective-permute-start | bytes 2359304 | tf_op jit(solution)/shard_map/ppermute | solution.py:478
  135.6 23.7 %collective-permute-start = (bf16[512,768]{1,0:T(8,128)(2,1)}, bf16[512,768]{1,0:T(8,128)(2,1)}, u32[]{:S(2)}, u32[]{:S(2)}) collective-permute-start(bf16[512,768]{1,0:T(8,128)(2,1)} %bitcast.11), channel_id=1, source_target_pairs={{0,2},{2,0},{1,3},{3,1},{4,6},{6,4},{5,7},{7,5},{8,10},{10,8},{9,1... | collective-permute-start | bytes 2359304 | tf_op jit(solution)/shard_map/ppermute | solution.py:478
  141.4 17.8 %copy-start.24 = (bf16[768,384]{1,0:T(8,128)(2,1)}, bf16[768,384]{1,0:T(8,128)(2,1)S(1)}, u32[]{:S(2)}) copy-start(bf16[768,384]{1,0:T(8,128)(2,1)S(1)} %get-tuple-element.101) | copy-start | bytes 1769476
  141.4 20.5 %copy-start.26 = (bf16[768,384]{1,0:T(8,128)(2,1)}, bf16[768,384]{1,0:T(8,128)(2,1)S(1)}, u32[]{:S(2)}) copy-start(bf16[768,384]{1,0:T(8,128)(2,1)S(1)} %get-tuple-element.102) | copy-start | bytes 1769476
  143.6 30.4 %copy-start.2 = (bf16[1024,768]{1,0:T(8,128)(2,1)}, bf16[1024,768]{1,0:T(8,128)(2,1)S(1)}, u32[]{:S(2)}) copy-start(bf16[1024,768]{1,0:T(8,128)(2,1)S(1)} %pad_maximum_fusion.6.ko_ref.vo_ref) | copy-start | bytes 4718596
  143.6 30.4 %collective-permute-start.3 = (bf16[1024,768]{1,0:T(8,128)(2,1)S(1)}, bf16[1024,768]{1,0:T(8,128)(2,1)S(1)}, u32[]{:S(2)}, u32[]{:S(2)}) collective-permute-start(bf16[1024,768]{1,0:T(8,128)(2,1)S(1)} %pad_maximum_fusion.6.ko_ref.vo_ref), channel_id=1, source_target_pairs={{0,1},{1,0},{2,3},{3,2},{4,5},{5,4},{6,7},{7,6},{8,9},{9,8},{10,11... | collective-permute-start | bytes 4718600 | tf_op jit(solution)/shard_map/ppermute | solution.py:486
  165.7 22.5 %collective-permute-start.1 = (bf16[1024,768]{1,0:T(8,128)(2,1)}, bf16[1024,768]{1,0:T(8,128)(2,1)}, u32[]{:S(2)}, u32[]{:S(2)}) collective-permute-start(bf16[1024,768]{1,0:T(8,128)(2,1)} %pad_maximum_fusion.4.ko_ref.vo_ref), channel_id=1, source_target_pairs={{0,1},{1,0},{2,3},{3,2},{4,5},{5,4},{6,7},{7,6},{8,9},{9,8},{10,11... | collective-permute-start | bytes 4718600 | tf_op jit(solution)/shard_map/ppermute | solution.py:486
  168.8 2.6 copy-start.28
  171.4 2.7 copy-start.17
  215.8 3.1 copy-start.22
  216.9 12.2 %collective-permute-start.4 = (bf16[512,384]{1,0:T(8,128)(2,1)}, bf16[512,384]{1,0:T(8,128)(2,1)}, u32[]{:S(2)}, u32[]{:S(2)}) collective-permute-start(bf16[512,384]{1,0:T(8,128)(2,1)} %get-tuple-element.112), channel_id=1, source_target_pairs={{0,2},{2,0},{1,3},{3,1},{4,6},{6,4},{5,7},{7,5},{8,10},{10,8},{9,1... | collective-permute-start | bytes 1179656 | tf_op jit(solution)/shard_map/ppermute | solution.py:488
  218.0 25.3 %collective-permute-start.5 = (bf16[512,384]{1,0:T(8,128)(2,1)}, bf16[512,384]{1,0:T(8,128)(2,1)}, u32[]{:S(2)}, u32[]{:S(2)}) collective-permute-start(bf16[512,384]{1,0:T(8,128)(2,1)} %get-tuple-element.122), channel_id=1, source_target_pairs={{0,2},{2,0},{1,3},{3,1},{4,6},{6,4},{5,7},{7,5},{8,10},{10,8},{9,1... | collective-permute-start | bytes 1179656 | tf_op jit(solution)/shard_map/ppermute | solution.py:488
  218.9 2.8 copy-start.30
  328.1 3.4 copy-start.31
  329.4 12.0 %collective-permute-start.6 = (bf16[512,384]{1,0:T(8,128)(2,1)S(1)}, bf16[512,384]{1,0:T(8,128)(2,1)S(1)}, u32[]{:S(2)}, u32[]{:S(2)}) collective-permute-start(bf16[512,384]{1,0:T(8,128)(2,1)S(1)} %get-tuple-element.110), channel_id=1, source_target_pairs={{0,2},{2,0},{1,3},{3,1},{4,6},{6,4},{5,7},{7,5},{8,10},{10,8},{9,1... | collective-permute-start | bytes 1179656 | tf_op jit(solution)/shard_map/ppermute | solution.py:496
  331.4 51.6 %collective-permute-start.9 = (bf16[512,384]{1,0:T(8,128)(2,1)S(1)}, bf16[512,384]{1,0:T(8,128)(2,1)S(1)}, u32[]{:S(2)}, u32[]{:S(2)}) collective-permute-start(bf16[512,384]{1,0:T(8,128)(2,1)S(1)} %get-tuple-element.111), channel_id=1, source_target_pairs={{0,2},{2,0},{1,3},{3,1},{4,6},{6,4},{5,7},{7,5},{8,10},{10,8},{9,1... | collective-permute-start | bytes 1179656 | tf_op jit(solution)/shard_map/ppermute | solution.py:496
  331.5 10.8 %copy-start.20 = (bf16[1024,384]{1,0:T(8,128)(2,1)S(1)}, bf16[1024,384]{1,0:T(8,128)(2,1)}, u32[]{:S(2)}) copy-start(bf16[1024,384]{1,0:T(8,128)(2,1)} %copy-done.19) | copy-start | bytes 2359300
  383.0 31.5 %collective-permute-start.7 = (bf16[1024,768]{1,0:T(8,128)(2,1)}, bf16[1024,768]{1,0:T(8,128)(2,1)}, u32[]{:S(2)}, u32[]{:S(2)}) collective-permute-start(bf16[1024,768]{1,0:T(8,128)(2,1)} %pad_maximum_fusion.7), channel_id=1, source_target_pairs={{0,1},{1,0},{2,3},{3,2},{4,5},{5,4},{6,7},{7,6},{8,9},{9,8},{10,11... | collective-permute-start | bytes 4718600 | tf_op jit(solution)/shard_map/ppermute | solution.py:501
  402.8 1.9 copy-start.15
  404.7 26.8 %collective-permute-start.10 = (bf16[1024,768]{1,0:T(8,128)(2,1)}, bf16[1024,768]{1,0:T(8,128)(2,1)}, u32[]{:S(2)}, u32[]{:S(2)}) collective-permute-start(bf16[1024,768]{1,0:T(8,128)(2,1)} %pad_maximum_fusion.8), channel_id=1, source_target_pairs={{0,1},{1,0},{2,3},{3,2},{4,5},{5,4},{6,7},{7,6},{8,9},{9,8},{10,11... | collective-permute-start | bytes 4718600 | tf_op jit(solution)/shard_map/ppermute | solution.py:501
  404.9 2.8 copy-start.25
  404.9 2.8 copy-start.27
  404.9 2.8 copy-start.29
  407.6 1.9 copy-start.41
  407.6 2.8 copy-start.40
  414.5 2.2 copy-start.8
  414.5 2.2 copy-start.10
  416.7 13.5 %copy-start.23 = (bf16[8,64,768]{2,1,0:T(8,128)(2,1)S(1)}, bf16[8,64,768]{2,1,0:T(8,128)(2,1)}, u32[]{:S(2)}) copy-start(bf16[8,64,768]{2,1,0:T(8,128)(2,1)} %copy-done.21) | copy-start | bytes 2359300
  416.7 13.5 %copy-start.33 = (bf16[512,768]{1,0:T(8,128)(2,1)S(1)}, bf16[512,768]{1,0:T(8,128)(2,1)}, u32[]{:S(2)}) copy-start(bf16[512,768]{1,0:T(8,128)(2,1)} %copy-done.32) | copy-start | bytes 2359300
  428.0 3.5 copy-start.12
  428.0 3.5 copy-start.14
  428.0 3.5 copy-start.16
  428.0 100.9 %collective-permute-start.8 = (bf16[512,768]{1,0:T(8,128)(2,1)}, bf16[512,768]{1,0:T(8,128)(2,1)}, u32[]{:S(2)}, u32[]{:S(2)}) collective-permute-start(bf16[512,768]{1,0:T(8,128)(2,1)} %get-tuple-element.69), channel_id=1, source_target_pairs={{0,2},{2,0},{1,3},{3,1},{4,6},{6,4},{5,7},{7,5},{8,10},{10,8},{9,1... | collective-permute-start | bytes 2359304 | tf_op jit(solution)/shard_map/ppermute | solution.py:505
  530.2 1.9 copy-start.39
  530.2 2.6 copy-start.38
  530.2 3.2 copy-start.37
  530.2 3.8 copy-start.36
  530.2 4.4 copy-start.35
  530.3 5.2 copy-start.34
  530.3 5.9 %copy-start.1 = (s32[16]{0:T(128)S(1)}, s32[16]{0:T(128)}, u32[]{:S(2)}) copy-start(s32[16]{0:T(128)} %param.20) | copy-start | bytes 196
  (11 other events, 14.1 us)
Sparse Core Ops, SparseCore 0:
  15.8 89.7 all-gather.3
  108.5 74.3 all-gather.5
  185.8 66.9 all-gather.7
